TPU v7x, 512 devices: a whole 4x4x16 slice. The times are simulated.
512 devices in a mesh: dp: 32 (over z, core), expert: 16 (over y, x).
Axes of the slice: x: 4, y: 4, z: 16, core: 2. Of those that a mesh axis runs over, the one named last changes fastest.
Arguments:
- tokens: bfloat16 [65536, 2048], P(('dp', 'expert')), may hold values from -24 to 24
- queries: bfloat16 [65536, 128], P(('dp', 'expert')), may hold values from -4.5 to 4.5
- key_vectors: bfloat16 [65536, 128], P(('dp', 'expert')), may hold values from -4.5 to 4.5
- gate_logits: float32 [65536, 32], P(('dp', 'expert')), may hold values from -6 to 6
- value_routes: int32 [65536, 2], P(('dp', 'expert')), may hold values from 0 to 15, all different within a row; in each aligned block of 128 rows (0 to 127, 128 to 255, ...) at most 20 rows name the same one
- output_routes: int32 [65536, 2], P(('dp', 'expert')), may hold values from 0 to 15, all different within a row; in each aligned block of 128 rows (0 to 127, 128 to 255, ...) at most 20 rows name the same one
- value_weight: bfloat16 [16, 2048, 128], P('expert', 'dp'), may hold values from -0.125 to 0.125
- output_weight: bfloat16 [16, 2048, 128], P('expert', 'dp'), may hold values from -0.5 to 0.5
- cotangent: bfloat16 [65536, 2048], P(('dp', 'expert')), may hold values from -24 to 24
Outputs:
- token_grad: bfloat16 [65536, 2048], P(('dp', 'expert'))
- query_grad: bfloat16 [65536, 128], P(('dp', 'expert'))
- key_grad: bfloat16 [65536, 128], P(('dp', 'expert'))
- logit_grad: float32 [65536, 32], P(('dp', 'expert'))
- value_weight_grad: float32 [16, 2048, 128], P('expert', 'dp')
- output_weight_grad: float32 [16, 2048, 128], P('expert', 'dp')
Inputs may be any that keep to these rules, and one draw needn't show every extreme that they name: `value_routes`: among one device's 128 tokens no value expert is named more than 20 times, a bound that some block reaches. `output_routes`: among one device's 128 tokens no output expert is named more than 20 times, a bound that some block reaches.
All inputs are finite; a program needn't handle non-finite values.
Results may differ from a plain program's by a relative error of at most 0.025.
Values may be sent and summed in bfloat16 or wider, within the bound.
A program may use at most 64 MiB of HBM per device.

v0:
```python
import math

import jax
import jax.numpy as jnp
from jax import lax
from jax.sharding import PartitionSpec as P


def slot_index(routes, experts, capacity):
    flattened = routes.reshape(-1)
    onehot = (flattened[:, None] == jnp.arange(experts, dtype=jnp.int32)[None, :]).astype(jnp.int32)
    before = jnp.cumsum(onehot, axis=0) - onehot
    return flattened * capacity + jnp.sum(before * onehot, axis=1)


def owner_rows(slots, experts, capacity):
    row_count = slots.shape[0]
    owner_table = jnp.full((experts * capacity,), row_count, jnp.int32)
    return owner_table.at[slots].set(jnp.arange(row_count, dtype=jnp.int32))


def causal_probs(queries, key_vectors):
    length_rows = queries.shape[0]
    scores = jnp.dot(queries, key_vectors.T, preferred_element_type=jnp.float32) / math.sqrt(
        queries.shape[1]
    )
    row_ids = lax.broadcasted_iota(jnp.int32, (length_rows, length_rows), 0)
    col_ids = lax.broadcasted_iota(jnp.int32, (length_rows, length_rows), 1)
    scores = jnp.where(row_ids >= col_ids, scores, -1e30)
    row_max = jnp.max(scores, axis=1, keepdims=True)
    exponent = jnp.exp(scores - row_max)
    return exponent / jnp.sum(exponent, axis=1, keepdims=True)


def to_owners(buffer):
    return lax.all_to_all(buffer, "expert", split_axis=0, concat_axis=0, tiled=True)


def from_owners(buffer):
    return lax.all_to_all(buffer, "expert", split_axis=0, concat_axis=0, tiled=True)


def transpose_product(left, right):
    return lax.dot_general(
        left, right, (((0,), (0,)), ((), ())), preferred_element_type=jnp.float32
    )


def on_device(
    tokens,
    queries,
    key_vectors,
    gate_logits,
    value_routes,
    output_routes,
    value_weight,
    output_weight,
    cotangent,
):
    tok_rows = tokens.shape[0]
    features = tokens.shape[1]
    head_size = queries.shape[1]
    experts = gate_logits.shape[1] // 2
    capacity = 5 * tok_rows // (2 * experts)
    groups = lax.axis_size("dp")
    gate_values = jax.nn.sigmoid(gate_logits)
    value_gate = jnp.take_along_axis(gate_values[:, :experts], value_routes, axis=1)
    output_gate = jnp.take_along_axis(gate_values[:, experts:], output_routes, axis=1)
    slot_value = slot_index(value_routes, experts, capacity)
    slot_output = slot_index(output_routes, experts, capacity)
    owner_value = owner_rows(slot_value, experts, capacity)
    owner_output = owner_rows(slot_output, experts, capacity)
    full_value, full_output = (
        lax.all_gather(value_weight, "dp", axis=1, tiled=True),
        lax.all_gather(output_weight, "dp", axis=1, tiled=True),
    )
    matrix_value = full_value[0]
    sent_tokens = jnp.take(tokens, owner_value // 2, axis=0, mode="fill", fill_value=0).reshape(
        experts, capacity, features
    )
    sent_grads = jnp.take(cotangent, owner_output // 2, axis=0, mode="fill", fill_value=0)
    held_tokens = to_owners(sent_tokens).reshape(experts * capacity, features)
    expert_out = jnp.dot(held_tokens, matrix_value, preferred_element_type=jnp.float32).astype(
        jnp.bfloat16
    )
    returned_value = from_owners(expert_out.reshape(experts, capacity, head_size)).reshape(
        experts * capacity, head_size
    )
    expert_value = returned_value[slot_value].reshape(tok_rows, 2, head_size).astype(jnp.float32)
    mixed_value = jnp.sum(value_gate[:, :, None] * expert_value, axis=1).astype(jnp.bfloat16)
    probs = causal_probs(queries, key_vectors)
    weights = probs.astype(jnp.bfloat16)
    hidden = jnp.dot(weights, mixed_value, preferred_element_type=jnp.float32).astype(jnp.bfloat16)
    gated_hidden = (
        (output_gate[:, :, None] * hidden[:, None, :].astype(jnp.float32))
        .astype(jnp.bfloat16)
        .reshape(2 * tok_rows, head_size)
    )
    sent_hidden = jnp.take(gated_hidden, owner_output, axis=0, mode="fill", fill_value=0)
    packed = jnp.concatenate([sent_grads, sent_hidden], axis=1).reshape(
        experts, capacity, features + head_size
    )
    held_output = to_owners(packed).reshape(experts * capacity, features + head_size)
    held_grads = held_output[:, :features]
    held_hidden = held_output[:, features:]
    matrix_output = full_output[0]
    head_rows = jnp.dot(held_grads, matrix_output, preferred_element_type=jnp.float32).astype(
        jnp.bfloat16
    )
    grad_output = transpose_product(held_grads, held_hidden)
    returned_output = from_owners(head_rows.reshape(experts, capacity, head_size)).reshape(
        experts * capacity, head_size
    )
    head_back = returned_output[slot_output].reshape(tok_rows, 2, head_size).astype(jnp.float32)
    output_gate_grad = jnp.sum(hidden[:, None, :].astype(jnp.float32) * head_back, axis=2)
    hidden_grad = jnp.sum(output_gate[:, :, None] * head_back, axis=1).astype(jnp.bfloat16)
    prob_grad = jnp.dot(hidden_grad, mixed_value.T, preferred_element_type=jnp.float32)
    score_grad = probs * (prob_grad - jnp.sum(prob_grad * probs, axis=1, keepdims=True))
    scaled_grad = (score_grad / math.sqrt(head_size)).astype(jnp.bfloat16)
    query_grad = jnp.dot(scaled_grad, key_vectors, preferred_element_type=jnp.float32).astype(
        jnp.bfloat16
    )
    key_grad = jnp.dot(scaled_grad.T, queries, preferred_element_type=jnp.float32).astype(
        jnp.bfloat16
    )
    value_grad = jnp.dot(weights.T, hidden_grad, preferred_element_type=jnp.float32).astype(
        jnp.bfloat16
    )
    gated_value = (
        (value_gate[:, :, None] * value_grad[:, None, :].astype(jnp.float32))
        .astype(jnp.bfloat16)
        .reshape(2 * tok_rows, head_size)
    )
    value_gate_grad = jnp.sum(value_grad[:, None, :].astype(jnp.float32) * expert_value, axis=2)
    sent_value = jnp.take(gated_value, owner_value, axis=0, mode="fill", fill_value=0).reshape(
        experts, capacity, head_size
    )
    held_value = to_owners(sent_value).reshape(experts * capacity, head_size)
    grad_value = transpose_product(held_tokens, held_value)
    token_rows_back = lax.dot_general(
        held_value, matrix_value, (((1,), (1,)), ((), ())), preferred_element_type=jnp.float32
    ).astype(jnp.bfloat16)
    returned_tokens = from_owners(token_rows_back.reshape(experts, capacity, features)).reshape(
        experts * capacity, features
    )
    token_grad = jnp.sum(
        returned_tokens[slot_value].reshape(tok_rows, 2, features).astype(jnp.float32), axis=1
    ).astype(jnp.bfloat16)
    summed_value, summed_output = (
        lax.psum_scatter(
            grad_value[None].astype(jnp.bfloat16), "dp", scatter_dimension=1, tiled=True
        ).astype(jnp.float32),
        lax.psum_scatter(
            grad_output[None].astype(jnp.bfloat16), "dp", scatter_dimension=1, tiled=True
        ).astype(jnp.float32),
    )
    value_weight_grad = summed_value / groups
    output_weight_grad = summed_output / groups
    expert_ids = jnp.arange(experts, dtype=jnp.int32)[None, None, :]
    hot_value = (value_routes[:, :, None] == expert_ids).astype(jnp.float32)
    hot_output = (output_routes[:, :, None] == expert_ids).astype(jnp.float32)
    logit_value = jnp.sum(
        hot_value * (value_gate_grad * value_gate * (1.0 - value_gate))[:, :, None], axis=1
    )
    logit_output = jnp.sum(
        hot_output * (output_gate_grad * output_gate * (1.0 - output_gate))[:, :, None], axis=1
    )
    logit_grad = jnp.concatenate([logit_value, logit_output], axis=1)
    return (token_grad, query_grad, key_grad, logit_grad, value_weight_grad, output_weight_grad)


def solution(mesh):
    in_specs = (
        P(("dp", "expert"), None),
        P(("dp", "expert"), None),
        P(("dp", "expert"), None),
        P(("dp", "expert"), None),
        P(("dp", "expert"), None),
        P(("dp", "expert"), None),
        P("expert", "dp", None),
        P("expert", "dp", None),
        P(("dp", "expert"), None),
    )
    out_specs = (
        P(("dp", "expert"), None),
        P(("dp", "expert"), None),
        P(("dp", "expert"), None),
        P(("dp", "expert"), None),
        P("expert", "dp", None),
        P("expert", "dp", None),
    )
    return jax.shard_map(
        on_device, mesh=mesh, in_specs=in_specs, out_specs=out_specs, check_vma=False
    )
```

profile of v0, /device:TPU:1, one launch (start us, length us, event | category | flops | bytes accessed | tf_op | source)
XLA Modules:
  0.0 382.1 jit_solution(1009859742498796397)
XLA Ops:
  7.2 0.7 broadcast_multiply_fusion
  7.9 0.8 copy.78
  10.2 1.4 scatter_custom_fusion.1
  12.1 2.4 gather_fusion.6
  14.7 1.3 reshape.211
  16.0 7.7 %all-to-all-start = ((bf16[16,20,2048]{2,1,0:T(8,128)(2,1)}), bf16[16,20,2048]{2,1,0:T(8,128)(2,1)S(1)}, u32[]{:S(2)}, u32[]{:S(2)}) async-start(bf16[16,20,2048]{2,1,0:T(8,128)(2,1)} %reshape.211), calls=%async_computation | async-start | bytes 3145728 | tf_op jit(solution)/shard_map/all_to_all | solution.py:36
  24.5 2.0 gather_fusion.4
  27.2 2.0 gather_fusion.3
  30.4 1.4 scatter_custom_fusion
  32.6 0.7 copy.83
  33.5 0.7 mul.144
  34.2 3.0 gather_fusion.5
  38.4 41.1 %all_gather.6 = bf16[1,2048,128]{2,1,0:T(8,128)(2,1)} all-gather(bf16[1,64,128]{2,1,0:T(8,128)(2,1)S(1)} %copy-done.19), channel_id=1, replica_groups=mesh['dp'=32,'expert'=16] {'dp'}, dimensions={1}, use_global_device_ids=true | all-gather | bytes 540672 | tf_op jit(solution)/shard_map/all_gather | solution.py:74
  79.5 1.5 broadcast_select_fusion.1
  81.0 1.4 reshape.212
  82.5 2.6 convolution_convert_fusion.2
  85.1 1.6 reshape.213
  86.7 7.1 %all-to-all-start.1 = ((bf16[16,20,128]{2,1,0:T(8,128)(2,1)}), bf16[16,20,128]{2,1,0:T(8,128)(2,1)S(1)}, u32[]{:S(2)}, u32[]{:S(2)}) async-start(bf16[16,20,128]{2,1,0:T(8,128)(2,1)} %reshape.213), calls=%async_computation.1 | async-start | bytes 196608 | tf_op jit(solution)/shard_map/all_to_all | solution.py:40
  93.8 6.7 %all-to-all-done.1 = bf16[16,20,128]{2,1,0:T(8,128)(2,1)S(1)} async-done(((bf16[16,20,128]{2,1,0:T(8,128)(2,1)}), bf16[16,20,128]{2,1,0:T(8,128)(2,1)S(1)}, u32[]{:S(2)}, u32[]{:S(2)}) %all-to-all-start.1) | async-done | bytes 81952 | tf_op jit(solution)/shard_map/all_to_all | solution.py:40
  100.4 1.0 gather_fusion
  101.4 1.1 fusion.15
  102.9 1.4 gather_fusion.7
  104.6 1.4 reshape.215
  106.0 3.8 %all-to-all-start.2 = ((bf16[16,20,2176]{2,1,0:T(8,128)(2,1)}), bf16[16,20,2176]{2,1,0:T(8,128)(2,1)S(1)}, u32[]{:S(2)}, u32[]{:S(2)}) async-start(bf16[16,20,2176]{2,1,0:T(8,128)(2,1)} %reshape.215), calls=%async_computation.2 | async-start | bytes 3342336 | tf_op jit(solution)/shard_map/all_to_all | solution.py:36
  110.0 29.7 %all_gather.7 = bf16[1,2048,128]{2,1,0:T(8,128)(2,1)S(1)} all-gather(bf16[1,64,128]{2,1,0:T(8,128)(2,1)S(1)} %copy-done.20), channel_id=1, replica_groups=mesh['dp'=32,'expert'=16] {'dp'}, dimensions={1}, use_global_device_ids=true | all-gather | bytes 540672 | tf_op jit(solution)/shard_map/all_gather | solution.py:75
  139.7 1.2 reshape.216
  140.9 1.9 fusion.6
  142.9 0.7 reshape.217
  143.5 6.9 %all-to-all-start.3 = ((bf16[16,20,128]{2,1,0:T(8,128)(2,1)}), bf16[16,20,128]{2,1,0:T(8,128)(2,1)S(1)}, u32[]{:S(2)}, u32[]{:S(2)}) async-start(bf16[16,20,128]{2,1,0:T(8,128)(2,1)} %reshape.217), calls=%async_computation.3 | async-start | bytes 196608 | tf_op jit(solution)/shard_map/all_to_all | solution.py:40
  150.7 1.4 fusion.2
  152.1 4.9 %all-to-all-done.3 = bf16[16,20,128]{2,1,0:T(8,128)(2,1)S(1)} async-done(((bf16[16,20,128]{2,1,0:T(8,128)(2,1)}), bf16[16,20,128]{2,1,0:T(8,128)(2,1)S(1)}, u32[]{:S(2)}, u32[]{:S(2)}) %all-to-all-start.3) | async-done | bytes 81952 | tf_op jit(solution)/shard_map/all_to_all | solution.py:40
  157.1 0.9 gather_fusion.1
  159.1 1.4 gather_fusion.8
  160.7 0.7 reshape.219
  161.3 3.5 all-to-all-start.4
  165.1 6.3 %all-to-all-done.4 = bf16[16,20,128]{2,1,0:T(8,128)(2,1)S(1)} async-done(((bf16[16,20,128]{2,1,0:T(8,128)(2,1)}), bf16[16,20,128]{2,1,0:T(8,128)(2,1)S(1)}, u32[]{:S(2)}, u32[]{:S(2)}) %all-to-all-start.4) | async-done | bytes 81952 | tf_op jit(solution)/shard_map/all_to_all | solution.py:36
  171.5 1.4 fusion.1
  173.5 1.3 reshape.221
  174.8 3.8 %all-to-all-start.5 = ((bf16[16,20,2048]{2,1,0:T(8,128)(2,1)}), bf16[16,20,2048]{2,1,0:T(8,128)(2,1)S(1)}, u32[]{:S(2)}, u32[]{:S(2)}) async-start(bf16[16,20,2048]{2,1,0:T(8,128)(2,1)} %reshape.221), calls=%async_computation.5 | async-start | bytes 3145728 | tf_op jit(solution)/shard_map/all_to_all | solution.py:40
  179.3 0.8 convolution_convert_fusion.3
  180.0 0.8 convolution_convert_fusion.4
  180.8 76.7 %reduce-scatter.5.cloned.1.call-done = bf16[1,64,128]{2,1,0:T(8,128)(2,1)} async-done(((bf16[1,2048,128]{2,1,0:T(8,128)(2,1)}), bf16[1,64,128]{2,1,0:T(8,128)(2,1)}) %reduce-scatter.5.cloned.1.call-update) | async-done | bytes 16400 | tf_op jit(solution)/shard_map/reduce_scatter | solution.py:153
  257.5 1.3 convert_multiply_fusion.4
  258.8 109.0 %reduce-scatter.3.cloned.1.call-done = bf16[1,64,128]{2,1,0:T(8,128)(2,1)} async-done(((bf16[1,2048,128]{2,1,0:T(8,128)(2,1)}), bf16[1,64,128]{2,1,0:T(8,128)(2,1)}) %reduce-scatter.3.cloned.1.call-update) | async-done | bytes 16400 | tf_op jit(solution)/shard_map/reduce_scatter | solution.py:150
  367.8 1.3 convert_multiply_fusion.5
  369.4 1.5 gather_fusion.2
  370.9 0.7 reshape.223
  371.7 3.6 reduce_sum.113
  (154 shorter events, 11.0 us)
Async XLA Ops:
  7.2 4.9 %copy-start = (bf16[128,2048]{1,0:T(8,128)(2,1)S(1)}, bf16[128,2048]{1,0:T(8,128)(2,1)}, u32[]{:S(2)}) copy-start(bf16[128,2048]{1,0:T(8,128)(2,1)} %param.15) | copy-start | bytes 1572868
  16.0 7.7 %copy-start.17 = (s32[128,2]{0,1:T(2,128)S(1)}, s32[128,2]{0,1:T(2,128)}, u32[]{:S(2)}) copy-start(s32[128,2]{0,1:T(2,128)} %param.19) | copy-start | bytes 3076
  16.0 7.7 %copy-start.18 = (s32[128,2]{0,1:T(2,128)S(1)}, s32[128,2]{0,1:T(2,128)}, u32[]{:S(2)}) copy-start(s32[128,2]{0,1:T(2,128)} %param.20) | copy-start | bytes 3076
  16.0 8.2 %copy-start.21 = (f32[128,32]{0,1:T(8,128)S(1)}, f32[128,32]{0,1:T(8,128)}, u32[]{:S(2)}) copy-start(f32[128,32]{0,1:T(8,128)} %param.18) | copy-start | bytes 49156
  16.0 64.9 %all-to-all-start = ((bf16[16,20,2048]{2,1,0:T(8,128)(2,1)}), bf16[16,20,2048]{2,1,0:T(8,128)(2,1)S(1)}, u32[]{:S(2)}, u32[]{:S(2)}) async-start(bf16[16,20,2048]{2,1,0:T(8,128)(2,1)} %reshape.211), calls=%async_computation | async-start | bytes 3145728 | tf_op jit(solution)/shard_map/all_to_all | solution.py:36
  27.2 5.2 %copy-start.11 = (bf16[128,128]{1,0:T(8,128)(2,1)S(1)}, bf16[128,128]{1,0:T(8,128)(2,1)}, u32[]{:S(2)}) copy-start(bf16[128,128]{1,0:T(8,128)(2,1)} %param.16) | copy-start | bytes 98308
  27.2 5.2 %copy-start.13 = (bf16[128,128]{1,0:T(8,128)(2,1)S(1)}, bf16[128,128]{1,0:T(8,128)(2,1)}, u32[]{:S(2)}) copy-start(bf16[128,128]{1,0:T(8,128)(2,1)} %param.17) | copy-start | bytes 98308
  29.2 5.0 %copy-start.1 = (bf16[128,2048]{1,0:T(8,128)(2,1)S(1)}, bf16[128,2048]{1,0:T(8,128)(2,1)}, u32[]{:S(2)}) copy-start(bf16[128,2048]{1,0:T(8,128)(2,1)} %param.23) | copy-start | bytes 1572868
  29.4 3.2 copy-start.22
  30.4 1.4 copy-start.28
  32.6 5.2 %copy-start.24 = (f32[128]{0:T(128)}, f32[128]{0:T(128)S(1)}, u32[]{:S(2)}) copy-start(f32[128]{0:T(128)S(1)} %get-tuple-element.19) | copy-start | bytes 1540
  33.5 3.7 copy-start.7
  34.2 4.2 %copy-start.19 = (bf16[1,64,128]{2,1,0:T(8,128)(2,1)S(1)}, bf16[1,64,128]{2,1,0:T(8,128)(2,1)}, u32[]{:S(2)}) copy-start(bf16[1,64,128]{2,1,0:T(8,128)(2,1)} %param.21) | copy-start | bytes 49156
  80.9 1.6 copy-start.2
  85.1 17.4 %copy-start.25 = (f32[128]{0:T(128)S(1)}, f32[128]{0:T(128)}, u32[]{:S(2)}) copy-start(f32[128]{0:T(128)} %copy-done.24) | copy-start | bytes 1540
  85.1 17.4 %copy-start.30 = (f32[128]{0:T(128)S(1)}, f32[128]{0:T(128)}, u32[]{:S(2)}) copy-start(f32[128]{0:T(128)} %fusion.21) | copy-start | bytes 1540
  85.1 17.7 %copy-start.27 = (f32[256]{0:T(256)S(1)}, f32[256]{0:T(256)}, u32[]{:S(2)}) copy-start(f32[256]{0:T(256)} %mul.144) | copy-start | bytes 3076
  86.7 17.7 %copy-start.33 = (pred[320]{0:T(512)(128)(4,1)S(1)}, pred[320]{0:T(512)(128)(4,1)}, u32[]{:S(2)}) copy-start(pred[320]{0:T(512)(128)(4,1)} %get-tuple-element.18) | copy-start | bytes 964
  86.7 13.7 %all-to-all-start.1 = ((bf16[16,20,128]{2,1,0:T(8,128)(2,1)}), bf16[16,20,128]{2,1,0:T(8,128)(2,1)S(1)}, u32[]{:S(2)}, u32[]{:S(2)}) async-start(bf16[16,20,128]{2,1,0:T(8,128)(2,1)} %reshape.213), calls=%async_computation.1 | async-start | bytes 196608 | tf_op jit(solution)/shard_map/all_to_all | solution.py:40
  102.5 1.8 copy-start.15
  102.7 1.6 copy-start.9
  106.0 3.9 %copy-start.6 = (f32[128,2]{1,0:T(8,128)S(1)}, f32[128,2]{1,0:T(8,128)}, u32[]{:S(2)}) copy-start(f32[128,2]{1,0:T(8,128)} %copy.83) | copy-start | bytes 3076
  106.0 4.0 %copy-start.29 = (s32[256,1]{0,1:T(1,128)S(1)}, s32[256,1]{0,1:T(1,128)}, u32[]{:S(2)}) copy-start(s32[256,1]{0,1:T(1,128)} %copy-done.28) | copy-start | bytes 3076
  106.0 4.0 %copy-start.20 = (bf16[1,64,128]{2,1,0:T(8,128)(2,1)S(1)}, bf16[1,64,128]{2,1,0:T(8,128)(2,1)}, u32[]{:S(2)}) copy-start(bf16[1,64,128]{2,1,0:T(8,128)(2,1)} %param.22) | copy-start | bytes 49156
  106.0 33.7 %all-to-all-start.2 = ((bf16[16,20,2176]{2,1,0:T(8,128)(2,1)}), bf16[16,20,2176]{2,1,0:T(8,128)(2,1)S(1)}, u32[]{:S(2)}, u32[]{:S(2)}) async-start(bf16[16,20,2176]{2,1,0:T(8,128)(2,1)} %reshape.215), calls=%async_computation.2 | async-start | bytes 3342336 | tf_op jit(solution)/shard_map/all_to_all | solution.py:36
  140.9 9.7 %copy-start.5 = (bf16[320,2176]{1,0:T(8,128)(2,1)S(1)}, bf16[320,2176]{1,0:T(8,128)(2,1)}, u32[]{:S(2)}) copy-start(bf16[320,2176]{1,0:T(8,128)(2,1)} %reshape.216) | copy-start | bytes 4177924
  143.5 13.5 %all-to-all-start.3 = ((bf16[16,20,128]{2,1,0:T(8,128)(2,1)}), bf16[16,20,128]{2,1,0:T(8,128)(2,1)S(1)}, u32[]{:S(2)}, u32[]{:S(2)}) async-start(bf16[16,20,128]{2,1,0:T(8,128)(2,1)} %reshape.217), calls=%async_computation.3 | async-start | bytes 196608 | tf_op jit(solution)/shard_map/all_to_all | solution.py:40
  150.4 7.6 %copy-start.8 = (f32[128,2]{1,0:T(8,128)S(1)}, f32[128,2]{1,0:T(8,128)}, u32[]{:S(2)}) copy-start(f32[128,2]{1,0:T(8,128)} %copy-done.7) | copy-start | bytes 3076
  150.4 7.6 %copy-start.10 = (f32[128,128]{1,0:T(8,128)S(1)}, f32[128,128]{1,0:T(8,128)}, u32[]{:S(2)}) copy-start(f32[128,128]{1,0:T(8,128)} %copy-done.9) | copy-start | bytes 196612
  150.4 107.1 %reduce-scatter.5.cloned.1.call-start = ((), (), s32[]{:S(2)}) async-start(), calls=%async_computation.9 | async-start | bytes 540672 | tf_op jit(solution)/shard_map/reduce_scatter | solution.py:153
  152.1 6.4 %copy-start.26 = (f32[128]{0:T(128)S(1)}, f32[128]{0:T(128)}, u32[]{:S(2)}) copy-start(f32[128]{0:T(128)} %copy-done.24) | copy-start | bytes 1540
  152.1 6.4 %copy-start.31 = (f32[128]{0:T(128)S(1)}, f32[128]{0:T(128)}, u32[]{:S(2)}) copy-start(f32[128]{0:T(128)} %fusion.21) | copy-start | bytes 1540
  157.1 3.5 copy-start.32
  158.0 7.0 %copy-start.23 = (f32[128,2]{0,1:T(2,128)S(1)}, f32[128,2]{0,1:T(2,128)}, u32[]{:S(2)}) copy-start(f32[128,2]{0,1:T(2,128)} %copy-done.22) | copy-start | bytes 3076
  158.0 7.0 %copy-start.16 = (bf16[128,128]{1,0:T(8,128)(2,1)S(1)}, bf16[128,128]{1,0:T(8,128)(2,1)}, u32[]{:S(2)}) copy-start(bf16[128,128]{1,0:T(8,128)(2,1)} %copy-done.15) | copy-start | bytes 98308
  158.4 13.0 %copy-start.3 = (bf16[16,20,2048]{2,1,0:T(8,128)(2,1)S(1)}, bf16[16,20,2048]{2,1,0:T(8,128)(2,1)}, u32[]{:S(2)}) copy-start(bf16[16,20,2048]{2,1,0:T(8,128)(2,1)} %copy-done.2) | copy-start | bytes 3932164
  161.3 10.1 %all-to-all-start.4 = ((bf16[16,20,128]{2,1,0:T(8,128)(2,1)}), bf16[16,20,128]{2,1,0:T(8,128)(2,1)S(1)}, u32[]{:S(2)}, u32[]{:S(2)}) async-start(bf16[16,20,128]{2,1,0:T(8,128)(2,1)} %reshape.219), calls=%async_computation.4 | async-start | bytes 196608 | tf_op jit(solution)/shard_map/all_to_all | solution.py:36
  164.8 202.9 %reduce-scatter.3.cloned.1.call-start = ((), (), s32[]{:S(2)}) async-start(), calls=%async_computation.8 | async-start | bytes 540672 | tf_op jit(solution)/shard_map/reduce_scatter | solution.py:150
  165.1 7.8 %copy-start.4 = (bf16[1,2048,128]{2,1,0:T(8,128)(2,1)S(1)}, bf16[1,2048,128]{2,1,0:T(8,128)(2,1)}, u32[]{:S(2)}) copy-start(bf16[1,2048,128]{2,1,0:T(8,128)(2,1)} %all_gather.6) | copy-start | bytes 1572868
  174.8 4.5 %copy-start.12 = (bf16[128,128]{1,0:T(8,128)(2,1)S(1)}, bf16[128,128]{1,0:T(8,128)(2,1)}, u32[]{:S(2)}) copy-start(bf16[128,128]{1,0:T(8,128)(2,1)} %param.16) | copy-start | bytes 98308
  174.8 5.2 %copy-start.14 = (bf16[128,128]{1,0:T(8,128)(2,1)S(1)}, bf16[128,128]{1,0:T(8,128)(2,1)}, u32[]{:S(2)}) copy-start(bf16[128,128]{1,0:T(8,128)(2,1)} %param.17) | copy-start | bytes 98308
  174.8 194.4 %all-to-all-start.5 = ((bf16[16,20,2048]{2,1,0:T(8,128)(2,1)}), bf16[16,20,2048]{2,1,0:T(8,128)(2,1)S(1)}, u32[]{:S(2)}, u32[]{:S(2)}) async-start(bf16[16,20,2048]{2,1,0:T(8,128)(2,1)} %reshape.221), calls=%async_computation.5 | async-start | bytes 3145728 | tf_op jit(solution)/shard_map/all_to_all | solution.py:40
Sparse Core Ops, SparseCore 0:
  154.0 103.4 reduce-scatter.4
  260.8 106.9 reduce-scatter.2
where the time goes:
time: 385 us; the launch traced here: 382 us
  waiting for transfers between devices  204 us (53%)
  blocking collectives  70.7 us (18%)
  local copies, waits for them, and re-layouts  34.4 us (9%)
  starting transfers between devices  33.1 us (9%)
  other arithmetic  15.4 us (4%)
  between operations  14.8 us (4%)
  matrix products  10.1 us (3%)
    reduce_scatter x1, waiting for transfers between devices, on_device(): lax.psum_scatter(grad_value[None].astype(jnp.bfloat16), 'dp', scatter_dim...  109 us
    reduce_scatter x1, waiting for transfers between devices, on_device(): lax.psum_scatter(grad_output[None].astype(jnp.bfloat16), 'dp', scatter_di...  76.7 us
    all_gather x1, blocking collectives, on_device(): lax.all_gather(value_weight, 'dp', axis=1, tiled=True)  41.1 us
    all_gather x1, blocking collectives, on_device(): lax.all_gather(output_weight, 'dp', axis=1, tiled=True)  29.7 us
    all_to_all x3, starting transfers between devices, from_owners(): lax.all_to_all(buffer, 'expert', split_axis=0, concat_axis=0, tiled=True)  17.8 us
    all_to_all x3, starting transfers between devices, to_owners(): lax.all_to_all(buffer, 'expert', split_axis=0, concat_axis=0, tiled=True)  15.1 us
    all_to_all x3, waiting for transfers between devices, from_owners(): lax.all_to_all(buffer, 'expert', split_axis=0, concat_axis=0, tiled=True)  11.6 us
  transfers between devices with their start and end apart: 8, of which 5 were waited for; matrix products, arithmetic and copies ran while one was open for 8% of the time, Pallas kernels for 0%

commit v1 on v0

v1 whole, which is shorter than its diff:
```python
import math

import jax
import jax.numpy as jnp
from jax import lax
from jax.sharding import PartitionSpec as P

BF16 = jnp.bfloat16
F32 = jnp.float32


def contract(left, right, dims):
    return lax.dot_general(left, right, (dims, ((), ())), preferred_element_type=F32)


def route_picks(routes, experts, stride, offset, width):
    rows = routes.shape[0]
    expert_ids = lax.broadcasted_iota(jnp.int32, (rows, experts), 1)
    hots = [(expert_ids == routes[:, k : k + 1]).astype(F32) for k in range(2)]
    row_ids = lax.broadcasted_iota(jnp.int32, (rows, rows), 0)
    col_ids = lax.broadcasted_iota(jnp.int32, (rows, rows), 1)
    earlier = (col_ids < row_ids).astype(BF16)
    rank = contract(earlier, (hots[0] + hots[1]).astype(BF16), ((1,), (0,)))
    place = rank + (expert_ids * stride + offset).astype(F32)
    slot_ids = lax.broadcasted_iota(jnp.int32, (rows, width), 1)
    picks = [
        (slot_ids == jnp.sum(hot * place, axis=1, keepdims=True).astype(jnp.int32)) for hot in hots
    ]
    return hots, [pick.astype(BF16) for pick in picks]


def attention_step(queries, keys, gate_logits, returned, value_hot, output_hot, value_pick, output_pick):
    rows, head_size = queries.shape
    experts = gate_logits.shape[1] // 2
    gates = jax.nn.sigmoid(gate_logits)
    value_gate = [jnp.sum(hot * gates[:, :experts], axis=1, keepdims=True) for hot in value_hot]
    output_gate = [jnp.sum(hot * gates[:, experts:], axis=1, keepdims=True) for hot in output_hot]
    expert_value = [contract(pick, returned, ((1,), (0,))) for pick in value_pick]
    head_back = [contract(pick, returned, ((1,), (0,))) for pick in output_pick]
    mixed_value = (value_gate[0] * expert_value[0] + value_gate[1] * expert_value[1]).astype(BF16)
    scores = contract(queries, keys, ((1,), (1,))) / math.sqrt(head_size)
    row_ids = lax.broadcasted_iota(jnp.int32, (rows, rows), 0)
    col_ids = lax.broadcasted_iota(jnp.int32, (rows, rows), 1)
    scores = jnp.where(row_ids >= col_ids, scores, -1e30)
    exponent = jnp.exp(scores - jnp.max(scores, axis=1, keepdims=True))
    probs = exponent / jnp.sum(exponent, axis=1, keepdims=True)
    weights = probs.astype(BF16)
    hidden = contract(weights, mixed_value, ((1,), (0,))).astype(BF16)
    hidden_wide = hidden.astype(F32)
    hidden_grad = (output_gate[0] * head_back[0] + output_gate[1] * head_back[1]).astype(BF16)
    prob_grad = contract(hidden_grad, mixed_value, ((1,), (1,)))
    score_grad = probs * (prob_grad - jnp.sum(prob_grad * probs, axis=1, keepdims=True))
    scaled_grad = (score_grad / math.sqrt(head_size)).astype(BF16)
    query_grad = contract(scaled_grad, keys, ((1,), (0,))).astype(BF16)
    key_grad = contract(scaled_grad, queries, ((0,), (0,))).astype(BF16)
    value_grad = contract(weights, hidden_grad, ((0,), (0,))).astype(BF16)
    value_wide = value_grad.astype(F32)
    gated_value = [(gate * value_wide).astype(BF16) for gate in value_gate]
    gated_hidden = [(gate * hidden_wide).astype(BF16) for gate in output_gate]
    logit_value = 0.0
    logit_output = 0.0
    for k in range(2):
        slope = jnp.sum(value_wide * expert_value[k], axis=1, keepdims=True)
        logit_value += value_hot[k] * (slope * value_gate[k] * (1.0 - value_gate[k]))
        slope = jnp.sum(hidden_wide * head_back[k], axis=1, keepdims=True)
        logit_output += output_hot[k] * (slope * output_gate[k] * (1.0 - output_gate[k]))
    logit_grad = jnp.concatenate([logit_value, logit_output], axis=1)
    sent_rows = contract(
        jnp.concatenate(value_pick + output_pick, axis=0),
        jnp.concatenate(gated_value + gated_hidden, axis=0),
        ((0,), (0,)),
    ).astype(BF16)
    return query_grad, key_grad, logit_grad, sent_rows


def exchange(rows, axis, count):
    blocks = rows.reshape(count, rows.shape[0] // count, rows.shape[1])
    return lax.all_to_all(blocks, axis, split_axis=0, concat_axis=0, tiled=True).reshape(rows.shape)


def on_device(
    tokens,
    queries,
    key_vectors,
    gate_logits,
    value_routes,
    output_routes,
    value_weight,
    output_weight,
    cotangent,
):
    tok_rows, features = tokens.shape
    head_size = queries.shape[1]
    experts = gate_logits.shape[1] // 2
    capacity = 5 * tok_rows // (2 * experts)
    stride = 2 * capacity
    slots = experts * stride
    groups = lax.axis_size("dp")
    half = features // 2
    shard = jnp.concatenate([value_weight[0], output_weight[0]], axis=1)
    banks = exchange(
        jnp.broadcast_to(shard[None], (groups,) + shard.shape).reshape(features, 2 * head_size), "dp", groups
    )
    value_hot, value_pick = route_picks(value_routes, experts, stride, 0, slots)
    output_hot, output_pick = route_picks(output_routes, experts, stride, capacity, slots)
    sent = contract(
        jnp.concatenate([value_pick[0] + value_pick[1], output_pick[0] + output_pick[1]], axis=0),
        jnp.concatenate([tokens, cotangent], axis=0),
        ((0,), (0,)),
    ).astype(BF16)
    held = exchange(sent, "expert", experts)
    slot_ids = lax.broadcasted_iota(jnp.int32, (slots, 1), 0) % stride
    is_value = slot_ids < capacity
    both = contract(held, banks, ((1,), (0,)))
    answer = jnp.where(is_value, both[:, :head_size], both[:, head_size:]).astype(BF16)
    returned = exchange(answer, "expert", experts)
    query_grad, key_grad, logit_grad, sent_rows = attention_step(
        queries, key_vectors, gate_logits, returned, value_hot, output_hot, value_pick, output_pick
    )
    held_rows = exchange(sent_rows, "expert", experts)
    zero = jnp.zeros_like(held_rows)
    wide_rows = jnp.concatenate(
        [jnp.where(is_value, held_rows, zero), jnp.where(is_value, zero, held_rows)], axis=1
    )
    partial = contract(held, wide_rows, ((0,), (0,))).astype(BF16)
    summed = exchange(partial, "dp", groups).reshape(groups, features // groups, 2 * head_size)
    summed = jnp.sum(summed.astype(F32), axis=0) / groups
    value_rows = held_rows.reshape(experts, stride, head_size)[:, :capacity]
    blank = jnp.zeros_like(value_rows)
    halves = jnp.concatenate(
        [jnp.concatenate([value_rows, blank], axis=1), jnp.concatenate([blank, value_rows], axis=1)], axis=2
    ).reshape(slots, 2 * head_size)
    half_banks = jnp.concatenate([banks[:half, :head_size], banks[half:, :head_size]], axis=1)
    back = contract(halves, half_banks, ((1,), (1,))).astype(BF16)
    back = exchange(back, "expert", experts)
    pick_low = value_pick[0] + value_pick[1]
    pick_high = jnp.concatenate([jnp.zeros((tok_rows, capacity), BF16), pick_low[:, :-capacity]], axis=1)
    token_grad = jnp.concatenate(
        [contract(pick, back, ((1,), (0,))).astype(BF16) for pick in (pick_low, pick_high)], axis=1
    )
    return (
        token_grad,
        query_grad,
        key_grad,
        logit_grad,
        summed[None, :, :head_size],
        summed[None, :, head_size:],
    )


def solution(mesh):
    rows = P(("dp", "expert"), None)
    bank = P("expert", "dp", None)
    return jax.shard_map(
        on_device,
        mesh=mesh,
        in_specs=(rows,) * 6 + (bank, bank, rows),
        out_specs=(rows,) * 4 + (bank, bank),
        check_vma=False,
    )
```

time: 385 us -> 245 us (0.64)
  blocking collectives: 70.7 us -> 0 us
  waiting for transfers between devices: 204 us -> 165 us
  local copies, waits for them, and re-layouts: 34.4 us -> 4.47 us
  starting transfers between devices: 33.1 us -> 50.5 us
  between operations: 14.8 us -> 1.04 us
  other arithmetic: 15.4 us -> 4.09 us
  matrix products: 10.1 us -> 18.9 us
    reduce_scatter x2 -> x0, waiting for transfers between devices: 186 us -> none  [the longest x1 109 us: on_device(): lax.psum_scatter(grad_value[None].astype(jnp.bfloat16), 'dp', scatter_dim...]
    all_to_all x6, waiting for transfers between devices: 17.9 us -> 165 us  [exchange(): lax.all_to_all(blocks, axis, split_axis=0, concat_axis=0, tiled=True)]
    all_gather x2 -> x0, blocking collectives: 70.7 us -> none  [the longest x1 41.1 us: on_device(): lax.all_gather(value_weight, 'dp', axis=1, tiled=True)]
    all_to_all x6, starting transfers between devices: 32.8 us -> 50.5 us  [exchange(): lax.all_to_all(blocks, axis, split_axis=0, concat_axis=0, tiled=True)]
    gather x17 -> x0, local copies, waits for them, and re-layouts: 16.4 us -> none  [the longest x1 3.01 us: on_device(): jnp.take(cotangent, owner_output // 2, axis=0, mode='fill', fill_value=0)]
    reshape x13 -> x0, local copies, waits for them, and re-layouts: 10.6 us -> none  [the longest x1 1.56 us: on_device(): expert_out.reshape(experts, capacity, head_size)]
    dot_general x11 -> x19, matrix products: 10.1 us -> 18.9 us  [contract(): lax.dot_general(left, right, (dims, ((), ())), preferred_element_type=F32)]
    reduce_sum x8 -> x2, other arithmetic: 6.12 us -> 0.2 us  [the longest x1 0.15 us: on_device(): summed = jnp.sum(summed.astype(F32), axis=0) / groups]
  transfers between devices with their start and end apart: 8 -> 6, of which waited for: 5 -> 6; matrix products, arithmetic and copies ran while one was open for 8% -> 4% of each run, Pallas kernels for 0% -> 0%
where the time goes in v1:
time: 245 us; the launch traced here: 244 us
  waiting for transfers between devices  165 us (67%)
  starting transfers between devices  50.5 us (21%)
  matrix products  18.9 us (8%)
  local copies, waits for them, and re-layouts  4.47 us (2%)
  other arithmetic  4.09 us (2%)
    all_to_all x6, waiting for transfers between devices, exchange(): lax.all_to_all(blocks, axis, split_axis=0, concat_axis=0, tiled=True)  165 us
    all_to_all x6, starting transfers between devices, exchange(): lax.all_to_all(blocks, axis, split_axis=0, concat_axis=0, tiled=True)  50.5 us
    dot_general x19, matrix products, contract(): lax.dot_general(left, right, (dims, ((), ())), preferred_element_type=F32)  18.9 us
  transfers between devices with their start and end apart: 6, of which 6 were waited for; matrix products, arithmetic and copies ran while one was open for 4% of the time, Pallas kernels for 0%

profile of v1, /device:TPU:1, one launch (start us, length us, event | category | flops | bytes accessed | tf_op | source)
XLA Modules:
  0.0 243.9 jit_solution(13930705491053911318)
XLA Ops:
  0.7 0.8 slice_bitcast_fusion.4
  1.4 0.8 slice_bitcast_fusion.3
  2.2 0.7 add_divide_fusion
  2.9 0.1 convolution_add_fusion.1
  3.0 0.6 select_reduce_fusion.5
  3.7 0.1 fusion.47
  3.8 0.1 fusion.48
  3.9 3.6 %convolution_convert_fusion = bf16[640,2048]{1,0:T(8,128)(2,1)} fusion(bf16[128,2048]{1,0:T(8,128)(2,1)} %param.17, bf16[128,2048]{1,0:T(8,128)(2,1)} %param.9, bf16[128,640]{1,0:T(8,128)(2,1)S(1)} %fusion.48, bf16[128,640]{1,0:T(8,128)(2,1)S(1)} %fusion.47), kind=kOutput, calls=%fused_computation | convolution fusion | flops 675151872 | bytes 3997696 | tf_op jit(solution)/shard_map/dot_general | solution.py:13
  7.5 7.7 %all-to-all-start = ((bf16[16,40,2048]{2,1,0:T(8,128)(2,1)}), bf16[16,40,2048]{2,1,0:T(8,128)(2,1)S(1)}, u32[]{:S(2)}, u32[]{:S(2)}) async-start(bf16[16,40,2048]{2,1,0:T(8,128)(2,1)} %bitcast.52), calls=%async_computation | async-start | bytes 5242880 | tf_op jit(solution)/shard_map/all_to_all | solution.py:78
  15.3 32.0 %all-to-all-done = bf16[16,40,2048]{2,1,0:T(8,128)(2,1)S(1)} async-done(((bf16[16,40,2048]{2,1,0:T(8,128)(2,1)}), bf16[16,40,2048]{2,1,0:T(8,128)(2,1)S(1)}, u32[]{:S(2)}, u32[]{:S(2)}) %all-to-all-start) | async-done | bytes 2621472 | tf_op jit(solution)/shard_map/all_to_all | solution.py:78
  47.3 1.2 broadcast_in_dim.32
  48.5 24.1 %all-to-all-start.1 = ((bf16[32,64,256]{2,1,0:T(8,128)(2,1)}), bf16[32,64,256]{2,1,0:T(8,128)(2,1)}, u32[]{:S(2)}, u32[]{:S(2)}) async-start(bf16[32,64,256]{2,1,0:T(8,128)(2,1)} %broadcast_in_dim.32), calls=%async_computation.1 | async-start | bytes 2097152 | tf_op jit(solution)/shard_map/all_to_all | solution.py:78
  72.6 0.1 fusion.30
  72.7 0.1 fusion.26
  72.8 55.4 %all-to-all-done.1 = bf16[32,64,256]{2,1,0:T(8,128)(2,1)} async-done(((bf16[32,64,256]{2,1,0:T(8,128)(2,1)}), bf16[32,64,256]{2,1,0:T(8,128)(2,1)}, u32[]{:S(2)}, u32[]{:S(2)}) %all-to-all-start.1) | async-done | bytes 1048608 | tf_op jit(solution)/shard_map/all_to_all | solution.py:78
  128.3 2.1 fusion.70
  130.4 0.8 fusion.18
  131.2 3.5 %all-to-all-start.2 = ((bf16[16,40,128]{2,1,0:T(8,128)(2,1)}), bf16[16,40,128]{2,1,0:T(8,128)(2,1)S(1)}, u32[]{:S(2)}, u32[]{:S(2)}) async-start(bf16[16,40,128]{2,1,0:T(8,128)(2,1)} %bitcast.9), calls=%async_computation.2 | async-start | bytes 327680 | tf_op jit(solution)/shard_map/all_to_all | solution.py:78
  134.7 0.2 fusion.69
  135.0 6.7 %all-to-all-done.2 = bf16[16,40,128]{2,1,0:T(8,128)(2,1)S(1)} async-done(((bf16[16,40,128]{2,1,0:T(8,128)(2,1)}), bf16[16,40,128]{2,1,0:T(8,128)(2,1)S(1)}, u32[]{:S(2)}, u32[]{:S(2)}) %all-to-all-start.2) | async-done | bytes 163872 | tf_op jit(solution)/shard_map/all_to_all | solution.py:78
  141.7 0.3 fusion.27
  142.0 0.3 fusion.29
  142.3 0.3 fusion.31
  142.6 0.3 add_convert_fusion.1
  142.9 1.4 multiply_reduce_fusion.3
  144.3 0.7 multiply_reduce_fusion.1
  145.0 1.0 convolution_convert_fusion.5
  146.1 3.5 %all-to-all-start.3 = ((bf16[16,40,128]{2,1,0:T(8,128)(2,1)}), bf16[16,40,128]{2,1,0:T(8,128)(2,1)S(1)}, u32[]{:S(2)}, u32[]{:S(2)}) async-start(bf16[16,40,128]{2,1,0:T(8,128)(2,1)} %bitcast.11), calls=%async_computation.3 | async-start | bytes 327680 | tf_op jit(solution)/shard_map/all_to_all | solution.py:78
  149.6 1.1 fusion.68
  150.7 5.9 %all-to-all-done.3 = bf16[16,40,128]{2,1,0:T(8,128)(2,1)S(1)} async-done(((bf16[16,40,128]{2,1,0:T(8,128)(2,1)}), bf16[16,40,128]{2,1,0:T(8,128)(2,1)S(1)}, u32[]{:S(2)}, u32[]{:S(2)}) %all-to-all-start.3) | async-done | bytes 163872 | tf_op jit(solution)/shard_map/all_to_all | solution.py:78
  156.6 0.1 broadcast_select_fusion
  156.7 0.1 fusion.17
  156.8 1.6 convolution_convert_fusion.2
  158.4 3.7 %all-to-all-start.4 = ((bf16[16,40,1024]{2,1,0:T(8,128)(2,1)}), bf16[16,40,1024]{2,1,0:T(8,128)(2,1)S(1)}, u32[]{:S(2)}, u32[]{:S(2)}) async-start(bf16[16,40,1024]{2,1,0:T(8,128)(2,1)} %bitcast.13), calls=%async_computation.4 | async-start | bytes 2621440 | tf_op jit(solution)/shard_map/all_to_all | solution.py:78
  162.1 0.2 bitcast_select_fusion.1
  162.3 3.8 %convolution_convert_fusion.1 = bf16[2048,256]{1,0:T(8,128)(2,1)} fusion(bf16[640,2048]{1,0:T(8,128)(2,1)} %bitcast.51, bf16[640,128]{1,0:T(8,128)(2,1)S(1)} %get-tuple-element.27, bf16[640,128]{1,0:T(8,128)(2,1)S(1)} %get-tuple-element.26), kind=kOutput, calls=%fused_computation.1 | convolution fusion | flops 672268288 | bytes 3997696 | tf_op jit(solution)/shard_map/dot_general | solution.py:13
  166.1 13.3 %all-to-all-done.4 = bf16[16,40,1024]{2,1,0:T(8,128)(2,1)S(1)} async-done(((bf16[16,40,1024]{2,1,0:T(8,128)(2,1)}), bf16[16,40,1024]{2,1,0:T(8,128)(2,1)S(1)}, u32[]{:S(2)}, u32[]{:S(2)}) %all-to-all-start.4) | async-done | bytes 1310752 | tf_op jit(solution)/shard_map/all_to_all | solution.py:78
  179.4 7.9 %all-to-all-start.5 = ((bf16[32,64,256]{2,1,0:T(8,128)(2,1)}), bf16[32,64,256]{2,1,0:T(8,128)(2,1)S(1)}, u32[]{:S(2)}, u32[]{:S(2)}) async-start(bf16[32,64,256]{2,1,0:T(8,128)(2,1)} %bitcast.16), calls=%async_computation.5 | async-start | bytes 2097152 | tf_op jit(solution)/shard_map/all_to_all | solution.py:78
  187.4 0.6 pad_maximum_fusion.2
  188.1 0.2 multiply_reduce_fusion.4
  188.3 0.8 convolution_convert_fusion.7
  189.1 0.8 convolution_convert_fusion.8
  189.9 0.4 convolution_convert_fusion.3
  190.3 0.4 convolution_convert_fusion.4
  190.7 0.8 pad_maximum_fusion
  191.6 51.5 %all-to-all-done.5 = bf16[32,64,256]{2,1,0:T(8,128)(2,1)S(1)} async-done(((bf16[32,64,256]{2,1,0:T(8,128)(2,1)}), bf16[32,64,256]{2,1,0:T(8,128)(2,1)S(1)}, u32[]{:S(2)}, u32[]{:S(2)}) %all-to-all-start.5) | async-done | bytes 1048608 | tf_op jit(solution)/shard_map/all_to_all | solution.py:78
  243.1 0.2 convert_reduce_fusion
  243.3 0.6 slice_bitcast_fusion
  (48 shorter events, 0.2 us)
Async XLA Ops:
  0.6 134.1 %copy-start = (bf16[128,128]{1,0:T(8,128)(2,1)S(1)}, bf16[128,128]{1,0:T(8,128)(2,1)}, u32[]{:S(2)}) copy-start(bf16[128,128]{1,0:T(8,128)(2,1)} %param.10) | copy-start | bytes 98308
  1.4 2.2 copy-start.5
  7.5 7.7 %copy-start.3 = (bf16[1,64,128]{2,1,0:T(8,128)(2,1)S(1)}, bf16[1,64,128]{2,1,0:T(8,128)(2,1)}, u32[]{:S(2)}) copy-start(bf16[1,64,128]{2,1,0:T(8,128)(2,1)} %param.16) | copy-start | bytes 49156
  7.5 7.7 %copy-start.4 = (bf16[1,64,128]{2,1,0:T(8,128)(2,1)S(1)}, bf16[1,64,128]{2,1,0:T(8,128)(2,1)}, u32[]{:S(2)}) copy-start(bf16[1,64,128]{2,1,0:T(8,128)(2,1)} %param.15) | copy-start | bytes 49156
  7.5 39.7 %all-to-all-start = ((bf16[16,40,2048]{2,1,0:T(8,128)(2,1)}), bf16[16,40,2048]{2,1,0:T(8,128)(2,1)S(1)}, u32[]{:S(2)}, u32[]{:S(2)}) async-start(bf16[16,40,2048]{2,1,0:T(8,128)(2,1)} %bitcast.52), calls=%async_computation | async-start | bytes 5242880 | tf_op jit(solution)/shard_map/all_to_all | solution.py:78
  47.3 83.1 %copy-start.1 = (bf16[16,40,2048]{2,1,0:T(8,128)(2,1)}, bf16[16,40,2048]{2,1,0:T(8,128)(2,1)S(1)}, u32[]{:S(2)}) copy-start(bf16[16,40,2048]{2,1,0:T(8,128)(2,1)S(1)} %all-to-all-done) | copy-start | bytes 7864324
  48.5 79.8 %all-to-all-start.1 = ((bf16[32,64,256]{2,1,0:T(8,128)(2,1)}), bf16[32,64,256]{2,1,0:T(8,128)(2,1)}, u32[]{:S(2)}, u32[]{:S(2)}) async-start(bf16[32,64,256]{2,1,0:T(8,128)(2,1)} %broadcast_in_dim.32), calls=%async_computation.1 | async-start | bytes 2097152 | tf_op jit(solution)/shard_map/all_to_all | solution.py:78
  128.3 6.5 %copy-start.2 = (bf16[128,128]{1,0:T(8,128)(2,1)S(1)}, bf16[128,128]{1,0:T(8,128)(2,1)}, u32[]{:S(2)}) copy-start(bf16[128,128]{1,0:T(8,128)(2,1)} %param.11) | copy-start | bytes 98308
  131.2 10.5 %all-to-all-start.2 = ((bf16[16,40,128]{2,1,0:T(8,128)(2,1)}), bf16[16,40,128]{2,1,0:T(8,128)(2,1)S(1)}, u32[]{:S(2)}, u32[]{:S(2)}) async-start(bf16[16,40,128]{2,1,0:T(8,128)(2,1)} %bitcast.9), calls=%async_computation.2 | async-start | bytes 327680 | tf_op jit(solution)/shard_map/all_to_all | solution.py:78
  144.3 6.4 %copy-start.14 = (bf16[128,128]{0,1:T(8,128)(2,1)}, bf16[128,128]{0,1:T(8,128)(2,1)S(1)}, u32[]{:S(2)}) copy-start(bf16[128,128]{0,1:T(8,128)(2,1)S(1)} %get-tuple-element.28) | copy-start | bytes 98308
  145.0 11.6 %copy-start.7 = (pred[40]{0:T(512)(128)(4,1)S(1)}, pred[40]{0:T(512)(128)(4,1)}, u32[]{:S(2)}) copy-start(pred[40]{0:T(512)(128)(4,1)} %constant.41.clone.1) | copy-start | bytes 124
  146.1 10.5 %all-to-all-start.3 = ((bf16[16,40,128]{2,1,0:T(8,128)(2,1)}), bf16[16,40,128]{2,1,0:T(8,128)(2,1)S(1)}, u32[]{:S(2)}, u32[]{:S(2)}) async-start(bf16[16,40,128]{2,1,0:T(8,128)(2,1)} %bitcast.11), calls=%async_computation.3 | async-start | bytes 327680 | tf_op jit(solution)/shard_map/all_to_all | solution.py:78
  158.4 21.0 %all-to-all-start.4 = ((bf16[16,40,1024]{2,1,0:T(8,128)(2,1)}), bf16[16,40,1024]{2,1,0:T(8,128)(2,1)S(1)}, u32[]{:S(2)}, u32[]{:S(2)}) async-start(bf16[16,40,1024]{2,1,0:T(8,128)(2,1)} %bitcast.13), calls=%async_computation.4 | async-start | bytes 2621440 | tf_op jit(solution)/shard_map/all_to_all | solution.py:78
  166.0 21.3 %copy-start.8 = (f32[128]{0:T(128)S(1)}, f32[128]{0:T(128)}, u32[]{:S(2)}) copy-start(f32[128]{0:T(128)} %get-tuple-element.18) | copy-start | bytes 1540
  166.0 21.3 %copy-start.9 = (f32[128]{0:T(128)S(1)}, f32[128]{0:T(128)}, u32[]{:S(2)}) copy-start(f32[128]{0:T(128)} %get-tuple-element.20) | copy-start | bytes 1540
  166.0 21.3 %copy-start.10 = (f32[128]{0:T(128)S(1)}, f32[128]{0:T(128)}, u32[]{:S(2)}) copy-start(f32[128]{0:T(128)} %get-tuple-element.6) | copy-start | bytes 1540
  166.0 21.3 %copy-start.11 = (f32[128]{0:T(128)S(1)}, f32[128]{0:T(128)}, u32[]{:S(2)}) copy-start(f32[128]{0:T(128)} %get-tuple-element.7) | copy-start | bytes 1540
  166.0 21.3 %copy-start.12 = (f32[128]{0:T(128)S(1)}, f32[128]{0:T(128)}, u32[]{:S(2)}) copy-start(f32[128]{0:T(128)} %get-tuple-element.8) | copy-start | bytes 1540
  166.0 21.3 %copy-start.13 = (f32[128]{0:T(128)S(1)}, f32[128]{0:T(128)}, u32[]{:S(2)}) copy-start(f32[128]{0:T(128)} %get-tuple-element.9) | copy-start | bytes 1540
  166.1 21.4 %copy-start.6 = (s32[128]{0:T(128)S(1)}, s32[128]{0:T(128)}, u32[]{:S(2)}) copy-start(s32[128]{0:T(128)} %copy-done.5) | copy-start | bytes 1540
  166.1 22.0 %copy-start.15 = (bf16[128,128]{0,1:T(8,128)(2,1)S(1)}, bf16[128,128]{0,1:T(8,128)(2,1)}, u32[]{:S(2)}) copy-start(bf16[128,128]{0,1:T(8,128)(2,1)} %copy-done.14) | copy-start | bytes 98308
  179.4 63.7 %all-to-all-start.5 = ((bf16[32,64,256]{2,1,0:T(8,128)(2,1)}), bf16[32,64,256]{2,1,0:T(8,128)(2,1)S(1)}, u32[]{:S(2)}, u32[]{:S(2)}) async-start(bf16[32,64,256]{2,1,0:T(8,128)(2,1)} %bitcast.16), calls=%async_computation.5 | async-start | bytes 2097152 | tf_op jit(solution)/shard_map/all_to_all | solution.py:78

commit v2 on v1

v2 whole, which is shorter than its diff:
```python
import functools
import math

import jax
import jax.numpy as jnp
from jax import lax
from jax.experimental import pallas as pl
from jax.experimental.pallas import tpu as pltpu
from jax.sharding import PartitionSpec as P

BF16 = jnp.bfloat16
F32 = jnp.float32
MESH = pl.DeviceIdType.MESH
SIDE = 4


def contract(left, right, dims):
    return lax.dot_general(left, right, (dims, ((), ())), preferred_element_type=F32)


def route_ranks(routes, experts):
    rows = routes.shape[0]
    expert_ids = lax.broadcasted_iota(jnp.int32, (rows, experts), 1)
    hots = [jnp.where(expert_ids == routes[:, k : k + 1], 1.0, 0.0).astype(F32) for k in range(2)]
    row_ids = lax.broadcasted_iota(jnp.int32, (rows, rows), 0)
    col_ids = lax.broadcasted_iota(jnp.int32, (rows, rows), 1)
    earlier = jnp.where(col_ids < row_ids, 1.0, 0.0).astype(BF16)
    rank = contract(earlier, (hots[0] + hots[1]).astype(BF16), ((1,), (0,)))
    places = [jnp.sum(hot * rank, axis=1, keepdims=True).astype(jnp.int32) for hot in hots]
    return hots, [routes[:, k : k + 1] for k in range(2)], places


def pick_rows(expert, place, stride, offset, width):
    slot_ids = lax.broadcasted_iota(jnp.int32, (expert.shape[0], width), 1)
    return jnp.where(slot_ids == expert * stride + place + offset, 1.0, 0.0).astype(F32)


def attention_step(queries, keys, gate_logits, returned, value_hot, output_hot, value_pick, output_pick):
    rows, head_size = queries.shape
    experts = gate_logits.shape[1] // 2
    gates = jax.nn.sigmoid(gate_logits)
    value_gate = [jnp.sum(hot * gates[:, :experts], axis=1, keepdims=True) for hot in value_hot]
    output_gate = [jnp.sum(hot * gates[:, experts:], axis=1, keepdims=True) for hot in output_hot]
    expert_value = [contract(pick, returned, ((1,), (0,))) for pick in value_pick]
    head_back = [contract(pick, returned, ((1,), (0,))) for pick in output_pick]
    mixed_value = (value_gate[0] * expert_value[0] + value_gate[1] * expert_value[1]).astype(BF16)
    scores = contract(queries, keys, ((1,), (1,))) / math.sqrt(head_size)
    row_ids = lax.broadcasted_iota(jnp.int32, (rows, rows), 0)
    col_ids = lax.broadcasted_iota(jnp.int32, (rows, rows), 1)
    scores = jnp.where(row_ids >= col_ids, scores, -1e30)
    exponent = jnp.exp(scores - jnp.max(scores, axis=1, keepdims=True))
    probs = exponent / jnp.sum(exponent, axis=1, keepdims=True)
    weights = probs.astype(BF16)
    hidden = contract(weights, mixed_value, ((1,), (0,))).astype(BF16)
    hidden_wide = hidden.astype(F32)
    hidden_grad = (output_gate[0] * head_back[0] + output_gate[1] * head_back[1]).astype(BF16)
    prob_grad = contract(hidden_grad, mixed_value, ((1,), (1,)))
    score_grad = probs * (prob_grad - jnp.sum(prob_grad * probs, axis=1, keepdims=True))
    scaled_grad = (score_grad / math.sqrt(head_size)).astype(BF16)
    query_grad = contract(scaled_grad, keys, ((1,), (0,))).astype(BF16)
    key_grad = contract(scaled_grad, queries, ((0,), (0,))).astype(BF16)
    value_grad = contract(weights, hidden_grad, ((0,), (0,))).astype(BF16)
    value_wide = value_grad.astype(F32)
    gated_value = [(gate * value_wide).astype(BF16) for gate in value_gate]
    gated_hidden = [(gate * hidden_wide).astype(BF16) for gate in output_gate]
    logit_value = 0.0
    logit_output = 0.0
    for k in range(2):
        slope = jnp.sum(value_wide * expert_value[k], axis=1, keepdims=True)
        logit_value += value_hot[k] * (slope * value_gate[k] * (1.0 - value_gate[k]))
        slope = jnp.sum(hidden_wide * head_back[k], axis=1, keepdims=True)
        logit_output += output_hot[k] * (slope * output_gate[k] * (1.0 - output_gate[k]))
    logit_grad = jnp.concatenate([logit_value, logit_output], axis=1)
    sent_rows = contract(
        jnp.concatenate(value_pick + output_pick, axis=0),
        jnp.concatenate(gated_value + gated_hidden, axis=0),
        ((0,), (0,)),
    ).astype(BF16)
    return query_grad, key_grad, logit_grad, sent_rows


def kernel(
    groups,
    tokens,
    queries,
    key_vectors,
    gate_logits,
    value_routes,
    output_routes,
    shard,
    cotangent,
    token_grad,
    query_grad,
    key_grad,
    logit_grad,
    value_weight_grad,
    output_weight_grad,
    sent,
    held,
    banks,
    quarter_bank,
    answer,
    returned,
    gated,
    held_rows,
    wide,
    spread,
    parts,
    pair,
    staged,
    landed,
    back,
    back_in,
    send_x,
    recv_x,
    send_z,
    recv_z,
    send_f,
    recv_f,
    send_p,
    recv_p,
    local,
):
    tok_rows, features = tokens.shape
    head_size = queries.shape[1]
    experts = gate_logits.shape[1] // 2
    capacity = 5 * tok_rows // (2 * experts)
    half, quarter = features // 2, features // 4
    chips = groups // 2
    shard_rows = features // groups
    block = 4 * capacity
    small = answer.shape[0] // experts
    me_dp = lax.axis_index("dp")
    me_ex = lax.axis_index("expert")
    z, core = me_dp // 2, me_dp % 2
    y, x = me_ex // SIDE, me_ex % SIDE
    partner = z * 2 + 1 - core

    def plane_peer(i):
        return ((y + i // SIDE) % SIDE) * SIDE + (x + i % SIDE) % SIDE

    def chip_step(j):
        return (j % 2) * ((j + 1) // 2) + (1 - j % 2) * (chips - j // 2)

    def chip_peer(j):
        return ((z + chip_step(j)) % chips) * 2 + core

    def chip_source(j):
        return ((z + chips - chip_step(j)) % chips) * 2 + core

    def window(ref, index, size):
        return ref.at[pl.ds(pl.multiple_of(index * size, 16), size)]

    def plane_copy(phase, source, target, size, i):
        peer = plane_peer(i)
        return pltpu.make_async_remote_copy(
            src_ref=window(source, peer, size),
            dst_ref=window(target, me_ex, size),
            send_sem=send_x.at[phase, i],
            recv_sem=recv_x.at[phase, i],
            device_id={"expert": peer},
            device_id_type=MESH,
        )

    def plane_own(phase, source, target, size):
        return pltpu.make_async_copy(
            window(source, me_ex, size), window(target, me_ex, size), local.at[phase]
        )

    def plane_start(phase, source, target, size):
        @pl.loop(1, experts)
        def _(i):
            plane_copy(phase, source, target, size, i).start()

        plane_own(phase, source, target, size).start()

    def plane_wait(phase, source, target, size):
        plane_own(phase, source, target, size).wait()

        @pl.loop(1, experts)
        def _(i):
            plane_copy(phase, source, target, size, i).wait_recv()

    def plane_drain(phase, source, target, size):
        @pl.loop(1, experts)
        def _(i):
            plane_copy(phase, source, target, size, i).wait_send()

    def shard_copy(j):
        return pltpu.make_async_remote_copy(
            src_ref=shard,
            dst_ref=window(banks, me_dp, shard_rows),
            send_sem=send_z.at[0, j],
            recv_sem=recv_z.at[0, j],
            device_id={"dp": chip_peer(j)},
            device_id_type=MESH,
        )

    def forward_copy(j, source, row):
        return pltpu.make_async_remote_copy(
            src_ref=source,
            dst_ref=window(banks, row, shard_rows),
            send_sem=send_f.at[j],
            recv_sem=recv_f.at[j],
            device_id={"dp": partner},
            device_id_type=MESH,
        )

    def forward_of(j):
        row = chip_source(j)
        return forward_copy(j, window(banks, row, shard_rows), row)

    def sum_copy(j):
        return pltpu.make_async_remote_copy(
            src_ref=staged.at[(z + chip_step(j)) % chips],
            dst_ref=landed.at[z],
            send_sem=send_z.at[1, j],
            recv_sem=recv_z.at[1, j],
            device_id={"dp": chip_peer(j)},
            device_id_type=MESH,
        )

    pair_copy = pltpu.make_async_remote_copy(
        src_ref=parts.at[1 - core],
        dst_ref=pair,
        send_sem=send_p,
        recv_sem=recv_p,
        device_id={"dp": partner},
        device_id_type=MESH,
    )

    barrier = pltpu.get_barrier_semaphore()

    @pl.loop(1, experts)
    def _(i):
        pl.semaphore_signal(barrier, inc=1, device_id={"expert": plane_peer(i)}, device_id_type=MESH)

    @pl.loop(1, chips)
    def _(j):
        pl.semaphore_signal(barrier, inc=1, device_id={"dp": chip_peer(j)}, device_id_type=MESH)

    pl.semaphore_signal(barrier, inc=1, device_id={"dp": partner}, device_id_type=MESH)

    own_shard = pltpu.make_async_copy(shard, window(banks, me_dp, shard_rows), local.at[4])
    own_shard.start()
    value_hot, value_expert, value_place = route_ranks(value_routes[...], experts)
    output_hot, output_expert, output_place = route_ranks(output_routes[...], experts)

    def pick_sum(expert, place, stride, offset, width):
        picks = [pick_rows(expert[k], place[k], stride, offset, width) for k in range(2)]
        return (picks[0] + picks[1]).astype(BF16)

    width = experts * block
    chosen = jnp.concatenate(
        [
            pick_sum(expert, place, block, offset, width)
            for expert, place, offset in (
                (value_expert, value_place, 0),
                (output_expert, output_place, capacity),
                (value_expert, value_place, 2 * capacity),
                (output_expert, output_place, 3 * capacity),
            )
        ],
        axis=0,
    )
    tile = 256
    cut = width // 2
    for c in range(half // tile):
        low = pl.ds(c * tile, tile)
        high = pl.ds(half + c * tile, tile)
        rows = jnp.concatenate([tokens[:, low], cotangent[:, low], tokens[:, high], cotangent[:, high]], axis=0)
        for part in range(2):
            sent[part * cut : (part + 1) * cut, low] = contract(
                chosen[:, part * cut : (part + 1) * cut], rows, ((0,), (0,))
            ).astype(BF16)

    pl.semaphore_wait(barrier, experts - 1 + chips)

    @pl.loop(1, chips)
    def _(j):
        shard_copy(j).start()

    plane_start(0, sent, held, block)
    forward_copy(0, shard, me_dp).start()

    @pl.loop(1, chips)
    def _(j):
        shard_copy(j).wait_recv()
        forward_of(j).start()

    own_shard.wait()

    @pl.loop(0, chips)
    def _(j):
        forward_of(j).wait_recv()

    bank_pair = jnp.concatenate([banks[:half, :], banks[half:, :]], axis=1)
    for q in range(4):
        quarter_bank[:, q * head_size : (q + 1) * head_size] = banks[q * quarter : (q + 1) * quarter, :head_size]

    plane_wait(0, sent, held, block)

    row_ids = lax.broadcasted_iota(jnp.int32, (2 * capacity, head_size), 0)
    chunk = 4
    for c in range(experts // chunk):
        both = contract(held[c * chunk * block : (c + 1) * chunk * block, :], bank_pair, ((1,), (0,)))
        for k in range(chunk):
            top = both[k * block : k * block + 2 * capacity, : 2 * head_size]
            low = both[k * block + 2 * capacity : (k + 1) * block, 2 * head_size :]
            total = top + low
            rows = jnp.where(row_ids < capacity, total[:, :head_size], total[:, head_size:])
            rows = jnp.concatenate([rows, jnp.zeros((small - 2 * capacity, head_size), F32)], axis=0)
            e = c * chunk + k
            answer[e * small : (e + 1) * small, :] = rows.astype(BF16)

    plane_start(1, answer, returned, small)
    value_pick = [
        pick_rows(value_expert[k], value_place[k], small, 0, experts * small).astype(BF16) for k in range(2)
    ]
    output_pick = [
        pick_rows(output_expert[k], output_place[k], small, capacity, experts * small).astype(BF16)
        for k in range(2)
    ]
    plane_wait(1, answer, returned, small)
    got = attention_step(
        queries[...],
        key_vectors[...],
        gate_logits[...],
        returned[...],
        value_hot,
        output_hot,
        value_pick,
        output_pick,
    )
    gated[...] = got[3]
    plane_start(2, gated, held_rows, small)
    query_grad[...] = got[0]
    key_grad[...] = got[1]
    logit_grad[...] = got[2]
    out_ids = lax.broadcasted_iota(jnp.int32, (block, small), 0)
    in_ids = lax.broadcasted_iota(jnp.int32, (block, small), 1)
    twice = out_ids - jnp.where(out_ids >= 2 * capacity, 2 * capacity, 0)
    fourfold = twice - jnp.where(twice >= capacity, capacity, 0)
    repeat_two = jnp.where(in_ids == twice, 1.0, 0.0).astype(BF16)
    repeat_four = jnp.where(in_ids == fourfold, 1.0, 0.0).astype(BF16)
    place_ids = lax.broadcasted_iota(jnp.int32, (block, head_size), 0)
    in_quarter = [
        (place_ids >= q * capacity) & (place_ids < (q + 1) * capacity) for q in range(4)
    ]
    plane_wait(2, gated, held_rows, small)
    for e in range(experts):
        rows = held_rows[e * small : (e + 1) * small, :]
        for repeat, target in ((repeat_two, wide), (repeat_four, spread)):
            copies = contract(repeat, rows, ((1,), (0,)))
            target[e * block : (e + 1) * block, :] = jnp.concatenate(
                [jnp.where(mask, copies, 0.0) for mask in in_quarter], axis=1
            ).astype(BF16)

    for c in range(half // tile):
        grads = contract(held[:, c * tile : (c + 1) * tile], wide[...], ((0,), (0,))).astype(BF16)
        for h in range(2):
            for s in range(tile // shard_rows):
                row = (h * half + c * tile) // shard_rows + s
                parts[row % 2, row // 2] = grads[
                    s * shard_rows : (s + 1) * shard_rows, h * 2 * head_size : (h + 1) * 2 * head_size
                ]
    pair_copy.start()
    for c in range(experts // chunk):
        span = slice(c * chunk * block, (c + 1) * chunk * block)
        back[span, :] = contract(spread[span, :], quarter_bank[...], ((1,), (1,))).astype(BF16)
    pair_copy.wait_recv()
    for k in range(chips):
        staged[k] = (parts[core, k].astype(F32) + pair[k].astype(F32)).astype(BF16)

    @pl.loop(1, chips)
    def _(j):
        sum_copy(j).start()

    plane_start(3, back, back_in, block)
    token_pick = [pick_sum(value_expert, value_place, block, q * capacity, width) for q in range(4)]
    plane_wait(3, back, back_in, block)
    for q in range(4):
        token_grad[:, q * quarter : (q + 1) * quarter] = contract(
            token_pick[q], back_in[...], ((1,), (0,))
        ).astype(BF16)

    landed[z] = staged[z]

    @pl.loop(1, chips)
    def _(j):
        sum_copy(j).wait_recv()

    total = landed[0].astype(F32)
    for k in range(1, chips):
        total = total + landed[k].astype(F32)
    total = total / groups
    value_weight_grad[...] = total[:, :head_size]
    output_weight_grad[...] = total[:, head_size:]

    plane_drain(0, sent, held, block)
    plane_drain(1, answer, returned, small)
    plane_drain(2, gated, held_rows, small)
    plane_drain(3, back, back_in, block)
    pair_copy.wait_send()

    @pl.loop(1, chips)
    def _(j):
        shard_copy(j).wait_send()
        sum_copy(j).wait_send()

    @pl.loop(0, chips)
    def _(j):
        forward_of(j).wait_send()


def on_device(
    tokens,
    queries,
    key_vectors,
    gate_logits,
    value_routes,
    output_routes,
    value_weight,
    output_weight,
    cotangent,
):
    tok_rows, features = tokens.shape
    head_size = queries.shape[1]
    experts = gate_logits.shape[1] // 2
    capacity = 5 * tok_rows // (2 * experts)
    groups = lax.axis_size("dp")
    chips = groups // 2
    shard_rows = features // groups
    small = 48
    block = 4 * capacity
    shard = jnp.concatenate([value_weight[0], output_weight[0]], axis=1)
    vmem = pl.BlockSpec(memory_space=pltpu.VMEM)

    def room(*shape):
        return pltpu.VMEM(shape, BF16)

    outs = pl.pallas_call(
        functools.partial(kernel, groups),
        out_shape=(
            jax.ShapeDtypeStruct((tok_rows, features), BF16),
            jax.ShapeDtypeStruct((tok_rows, head_size), BF16),
            jax.ShapeDtypeStruct((tok_rows, head_size), BF16),
            jax.ShapeDtypeStruct((tok_rows, 2 * experts), F32),
            jax.ShapeDtypeStruct((shard_rows, head_size), F32),
            jax.ShapeDtypeStruct((shard_rows, head_size), F32),
        ),
        in_specs=[vmem] * 8,
        out_specs=(vmem,) * 6,
        scratch_shapes=[
            room(experts * block, features // 2),
            room(experts * block, features // 2),
            room(features, 2 * head_size),
            room(features // 4, 4 * head_size),
            room(experts * small, head_size),
            room(experts * small, head_size),
            room(experts * small, head_size),
            room(experts * small, head_size),
            room(experts * block, 4 * head_size),
            room(experts * block, 4 * head_size),
            room(2, chips, shard_rows, 2 * head_size),
            room(chips, shard_rows, 2 * head_size),
            room(chips, shard_rows, 2 * head_size),
            room(chips, shard_rows, 2 * head_size),
            room(experts * block, features // 4),
            room(experts * block, features // 4),
            pltpu.SemaphoreType.DMA((4, experts)),
            pltpu.SemaphoreType.DMA((4, experts)),
            pltpu.SemaphoreType.DMA((2, chips)),
            pltpu.SemaphoreType.DMA((2, chips)),
            pltpu.SemaphoreType.DMA((chips,)),
            pltpu.SemaphoreType.DMA((chips,)),
            pltpu.SemaphoreType.DMA,
            pltpu.SemaphoreType.DMA,
            pltpu.SemaphoreType.DMA((5,)),
        ],
        compiler_params=pltpu.CompilerParams(collective_id=0, has_side_effects=True),
    )(tokens, queries, key_vectors, gate_logits, value_routes, output_routes, shard, cotangent)
    return outs[:4] + (outs[4][None], outs[5][None])


def solution(mesh):
    rows = P(("dp", "expert"), None)
    bank = P("expert", "dp", None)
    return jax.shard_map(
        on_device,
        mesh=mesh,
        in_specs=(rows,) * 6 + (bank, bank, rows),
        out_specs=(rows,) * 4 + (bank, bank),
        check_vma=False,
    )
```

time: 245 us -> 119 us (0.49)
  waiting for transfers between devices: 165 us -> 0 us
  Pallas kernels: 0 us -> 108 us
  starting transfers between devices: 50.5 us -> 0 us
  matrix products: 18.9 us -> 0 us
  local copies, waits for them, and re-layouts: 4.47 us -> 8.53 us
  other arithmetic: 4.09 us -> 1.36 us
    all_to_all x6 -> x0, waiting for transfers between devices: 165 us -> none  [exchange(): lax.all_to_all(blocks, axis, split_axis=0, concat_axis=0, tiled=True)]
    pallas_call x0 -> x1, Pallas kernels: none -> 108 us  [on_device(): pl.pallas_call(functools.partial(kernel, groups), out_shape=(jax.ShapeDty...]
    all_to_all x6 -> x0, starting transfers between devices: 50.5 us -> none  [exchange(): lax.all_to_all(blocks, axis, split_axis=0, concat_axis=0, tiled=True)]
    dot_general x19 -> x0, matrix products: 18.9 us -> none  [contract(): lax.dot_general(left, right, (dims, ((), ())), preferred_element_type=F32)]
    unnamed x32 -> x23, local copies, waits for them, and re-layouts: 0.07 us -> 8.53 us
  transfers between devices with their start and end apart: 6 -> 0, of which waited for: 6 -> 0; matrix products, arithmetic and copies ran while one was open for 4% -> 0% of each run, Pallas kernels for 0% -> 0%
where the time goes in v2:
time: 119 us; the launch traced here: 118 us
  Pallas kernels  108 us (91%)
  local copies, waits for them, and re-layouts  8.53 us (7%)
  other arithmetic  1.36 us (1%)
    pallas_call x1, Pallas kernels, on_device(): pl.pallas_call(functools.partial(kernel, groups), out_shape=(jax.ShapeDty...  108 us
    unnamed x23, local copies, waits for them, and re-layouts  8.53 us

profile of v2, /device:TPU:1, one launch (start us, length us, event | category | flops | bytes accessed | tf_op | source)
XLA Modules:
  0.0 118.3 jit_solution(12416221936605437688)
XLA Ops:
  0.6 0.0 copy-start.4
  0.6 1.4 %pad_maximum_fusion.shard = bf16[64,256]{1,0:T(8,128)(2,1)} fusion(bf16[64,128]{1,0:T(8,128)(2,1)} %bitcast.6, bf16[64,128]{1,0:T(8,128)(2,1)} %bitcast.7), kind=kLoop, calls=%fused_computation | loop fusion | flops 65536 | bytes 65536 | tf_op jit(solution)/shard_map/concatenate | solution.py:436
  2.0 0.0 copy-done.4
  2.0 0.0 copy-start.5
  2.0 0.7 copy.15.gate_logits
  2.7 0.0 copy-done.5
  2.7 0.0 copy-start.6
  2.7 0.7 copy.16.value_routes
  3.5 0.0 copy-done.6
  3.5 0.7 copy.17.output_routes
  4.2 107.8 %shard_map.136 = (bf16[128,2048]{1,0:T(8,128)(2,1)}, bf16[128,128]{1,0:T(8,128)(2,1)}, bf16[128,128]{1,0:T(8,128)(2,1)}, f32[128,32]{1,0:T(8,128)}, f32[64,128]{1,0:T(8,128)}, /*index=5*/f32[64,128]{1,0:T(8,128)}) custom-call(bf16[128,2048]{1,0:T(8,128)(2,1)} %tokens.1, bf16[128,128]{1,0:T(8,128)(2,1)} %queries.1, bf16[128,128]{1,0:T(8,128)(2,1)} %key_vectors.1, ...), custom_call_target="tpu_custom_call" | custom-call | tf_op jit(solution)/shard_map/pallas_call | solution.py:442
  112.0 1.5 %copy.18 = f32[128,32]{0,1:T(8,128)} copy(f32[128,32]{1,0:T(8,128)} %get-tuple-element.21) | data formatting | bytes 32768
  113.5 0.0 copy-start.3
  113.5 1.9 %copy.24 = bf16[128,2048]{1,0:T(8,128)(2,1)} copy(bf16[128,2048]{1,0:T(8,128)(2,1)} %get-tuple-element.30) | data formatting | bytes 1048576
  115.4 0.0 copy-done.3
  115.4 0.0 copy-start.2
  115.4 0.6 copy.25
  116.0 0.2 copy-done.2
  116.2 0.0 copy-start.1
  116.2 0.6 copy.26
  116.8 0.2 copy-done.1
  117.0 0.0 copy-start
  117.0 0.6 copy.27
  117.6 0.2 copy-done
  117.7 0.6 copy.28
Async XLA Ops:
  0.6 1.4 %copy-start.4 = (f32[128,32]{0,1:T(8,128)S(1)}, f32[128,32]{0,1:T(8,128)}, u32[]{:S(2)}) copy-start(f32[128,32]{0,1:T(8,128)} %param.12) | copy-start | bytes 49156
  2.0 0.7 copy-start.5
  2.7 0.7 copy-start.6
  113.5 1.9 %copy-start.3 = (bf16[128,128]{1,0:T(8,128)(2,1)S(1)}, bf16[128,128]{1,0:T(8,128)(2,1)}, u32[]{:S(2)}) copy-start(bf16[128,128]{1,0:T(8,128)(2,1)} %get-tuple-element.31) | copy-start | bytes 98308
  115.4 0.8 copy-start.2
  116.2 0.8 copy-start.1
  117.0 0.8 copy-start

commit v3 on v2

--- a/solution.py
+++ b/solution.py
@@ -12,6 +12,12 @@
 F32 = jnp.float32
 MESH = pl.DeviceIdType.MESH
 SIDE = 4
+RELAYED = (
+    ((1, 2), (0, 3), (1, 3)),
+    ((3, 2), (0, 3), (3, 3)),
+    ((2, 1), (3, 1), (3, 0)),
+    ((2, 3), (3, 3), (3, 0)),
+)
 
 
 def contract(left, right, dims):
@@ -19,20 +25,26 @@
 
 
 def route_ranks(routes, experts):
-    rows = routes.shape[0]
-    expert_ids = lax.broadcasted_iota(jnp.int32, (rows, experts), 1)
-    hots = [jnp.where(expert_ids == routes[:, k : k + 1], 1.0, 0.0).astype(F32) for k in range(2)]
-    row_ids = lax.broadcasted_iota(jnp.int32, (rows, rows), 0)
-    col_ids = lax.broadcasted_iota(jnp.int32, (rows, rows), 1)
-    earlier = jnp.where(col_ids < row_ids, 1.0, 0.0).astype(BF16)
-    rank = contract(earlier, (hots[0] + hots[1]).astype(BF16), ((1,), (0,)))
-    places = [jnp.sum(hot * rank, axis=1, keepdims=True).astype(jnp.int32) for hot in hots]
-    return hots, [routes[:, k : k + 1] for k in range(2)], places
+    tokens = routes.shape[1]
+    expert_ids = lax.broadcasted_iota(jnp.int32, (experts, tokens), 0)
+    hots = [jnp.where(expert_ids == routes[k : k + 1, :], 1.0, 0.0).astype(F32) for k in range(2)]
+    row_ids = lax.broadcasted_iota(jnp.int32, (tokens, tokens), 0)
+    col_ids = lax.broadcasted_iota(jnp.int32, (tokens, tokens), 1)
+    earlier = jnp.where(row_ids < col_ids, 1.0, 0.0).astype(BF16)
+    rank = contract((hots[0] + hots[1]).astype(BF16), earlier, ((1,), (0,)))
+    places = [jnp.sum(hot * rank, axis=0, keepdims=True) for hot in hots]
+    return [routes[k : k + 1, :].astype(F32) for k in range(2)] + places
 
 
 def pick_rows(expert, place, stride, offset, width):
     slot_ids = lax.broadcasted_iota(jnp.int32, (expert.shape[0], width), 1)
     return jnp.where(slot_ids == expert * stride + place + offset, 1.0, 0.0).astype(F32)
+
+
+def chosen_rows(expert, place, stride, offset, width):
+    slot_ids = lax.broadcasted_iota(jnp.int32, (width, expert[0].shape[1]), 0)
+    slots = [(expert[k] * stride + place[k] + offset).astype(jnp.int32) for k in range(2)]
+    return jnp.where((slot_ids == slots[0]) | (slot_ids == slots[1]), 1.0, 0.0).astype(BF16)
 
 
 def attention_step(queries, keys, gate_logits, returned, value_hot, output_hot, value_pick, output_pick):
@@ -87,7 +99,8 @@
     gate_logits,
     value_routes,
     output_routes,
-    shard,
+    value_weight,
+    output_weight,
     cotangent,
     token_grad,
     query_grad,
@@ -95,8 +108,11 @@
     logit_grad,
     value_weight_grad,
     output_weight_grad,
+    shard,
     sent,
     held,
+    relay,
+    back_relay,
     banks,
     quarter_bank,
     answer,
@@ -119,11 +135,13 @@
     recv_f,
     send_p,
     recv_p,
+    send_r,
+    recv_r,
     local,
 ):
     tok_rows, features = tokens.shape
     head_size = queries.shape[1]
-    experts = gate_logits.shape[1] // 2
+    experts = gate_logits.shape[0] // 2
     capacity = 5 * tok_rows // (2 * experts)
     half, quarter = features // 2, features // 4
     chips = groups // 2
@@ -181,6 +199,50 @@
         def _(i):
             plane_copy(phase, source, target, size, i).wait_recv()
 
+    def step(dy, dx):
+        return ((y + dy) % SIDE) * SIDE + (x + dx) % SIDE
+
+    def first_leg(phase, source, buffer, size, r):
+        (dy, dx), via, _ = RELAYED[r]
+        return pltpu.make_async_remote_copy(
+            src_ref=window(source, step(dy, dx), size),
+            dst_ref=buffer.at[r],
+            send_sem=send_x.at[phase, dy * SIDE + dx],
+            recv_sem=recv_r.at[phase // 3, r],
+            device_id={"expert": step(*via)},
+            device_id_type=MESH,
+        )
+
+    def last_leg(phase, buffer, target, size, r):
+        (dy, dx), via, leg = RELAYED[r]
+        return pltpu.make_async_remote_copy(
+            src_ref=buffer.at[r],
+            dst_ref=window(target, step(SIDE - via[0], SIDE - via[1]), size),
+            send_sem=send_r.at[phase // 3, r],
+            recv_sem=recv_x.at[phase, dy * SIDE + dx],
+            device_id={"expert": step(*leg)},
+            device_id_type=MESH,
+        )
+
+    direct = [i for i in range(1, SIDE * SIDE) if (i // SIDE, i % SIDE) not in [r[0] for r in RELAYED]]
+
+    def balanced_start(phase, source, buffer, target, size):
+        for r in range(len(RELAYED)):
+            first_leg(phase, source, buffer, size, r).start()
+        for i in sorted(direct, key=lambda i: -(i // SIDE == 2) - (i % SIDE == 2)):
+            plane_copy(phase, source, target, size, i).start()
+        plane_own(phase, source, target, size).start()
+
+    def balanced_relay(phase, source, buffer, target, size):
+        for r in range(len(RELAYED)):
+            first_leg(phase, source, buffer, size, r).wait_recv()
+            last_leg(phase, buffer, target, size, r).start()
+
+    def balanced_drain(phase, source, buffer, target, size):
+        plane_drain(phase, source, target, size)
+        for r in range(len(RELAYED)):
+            last_leg(phase, buffer, target, size, r).wait_send()
+
     def plane_drain(phase, source, target, size):
         @pl.loop(1, experts)
         def _(i):
@@ -241,27 +303,24 @@
 
     pl.semaphore_signal(barrier, inc=1, device_id={"dp": partner}, device_id_type=MESH)
 
+    shard[:, :head_size] = value_weight[0]
+    shard[:, head_size:] = output_weight[0]
     own_shard = pltpu.make_async_copy(shard, window(banks, me_dp, shard_rows), local.at[4])
     own_shard.start()
-    value_hot, value_expert, value_place = route_ranks(value_routes[...], experts)
-    output_hot, output_expert, output_place = route_ranks(output_routes[...], experts)
-
-    def pick_sum(expert, place, stride, offset, width):
-        picks = [pick_rows(expert[k], place[k], stride, offset, width) for k in range(2)]
-        return (picks[0] + picks[1]).astype(BF16)
-
+    value_stats = route_ranks(value_routes[...], experts)
+    output_stats = route_ranks(output_routes[...], experts)
     width = experts * block
     chosen = jnp.concatenate(
         [
-            pick_sum(expert, place, block, offset, width)
-            for expert, place, offset in (
-                (value_expert, value_place, 0),
-                (output_expert, output_place, capacity),
-                (value_expert, value_place, 2 * capacity),
-                (output_expert, output_place, 3 * capacity),
+            chosen_rows(stats[:2], stats[2:], block, offset, width)
+            for stats, offset in (
+                (value_stats, 0),
+                (output_stats, capacity),
+                (value_stats, 2 * capacity),
+                (output_stats, 3 * capacity),
             )
         ],
-        axis=0,
+        axis=1,
     )
     tile = 256
     cut = width // 2
@@ -271,17 +330,32 @@
         rows = jnp.concatenate([tokens[:, low], cotangent[:, low], tokens[:, high], cotangent[:, high]], axis=0)
         for part in range(2):
             sent[part * cut : (part + 1) * cut, low] = contract(
-                chosen[:, part * cut : (part + 1) * cut], rows, ((0,), (0,))
+                chosen[part * cut : (part + 1) * cut, :], rows, ((1,), (0,))
             ).astype(BF16)
 
     pl.semaphore_wait(barrier, experts - 1 + chips)
+    balanced_start(0, sent, relay, held, block)
 
     @pl.loop(1, chips)
     def _(j):
         shard_copy(j).start()
 
-    plane_start(0, sent, held, block)
     forward_copy(0, shard, me_dp).start()
+    columns = jnp.concatenate(value_stats + output_stats, axis=0).T.astype(jnp.int32)
+    value_expert, value_place, output_expert, output_place = [
+        [columns[:, 2 * n + k : 2 * n + k + 1] for k in range(2)] for n in range(4)
+    ]
+    expert_ids = lax.broadcasted_iota(jnp.int32, (tok_rows, experts), 1)
+    value_hot, output_hot = [
+        [jnp.where(expert_ids == column, 1.0, 0.0).astype(F32) for column in pair_of]
+        for pair_of in (value_expert, output_expert)
+    ]
+
+    def pick_sum(expert, place, stride, offset, width):
+        picks = [pick_rows(expert[k], place[k], stride, offset, width) for k in range(2)]
+        return (picks[0] + picks[1]).astype(BF16)
+
+    balanced_relay(0, sent, relay, held, block)
 
     @pl.loop(1, chips)
     def _(j):
@@ -325,7 +399,7 @@
     got = attention_step(
         queries[...],
         key_vectors[...],
-        gate_logits[...],
+        gate_logits[...].T,
         returned[...],
         value_hot,
         output_hot,
@@ -336,7 +410,7 @@
     plane_start(2, gated, held_rows, small)
     query_grad[...] = got[0]
     key_grad[...] = got[1]
-    logit_grad[...] = got[2]
+    logit_grad[...] = got[2].T
     out_ids = lax.broadcasted_iota(jnp.int32, (block, small), 0)
     in_ids = lax.broadcasted_iota(jnp.int32, (block, small), 1)
     twice = out_ids - jnp.where(out_ids >= 2 * capacity, 2 * capacity, 0)
@@ -376,7 +450,8 @@
     def _(j):
         sum_copy(j).start()
 
-    plane_start(3, back, back_in, block)
+    balanced_start(3, back, back_relay, back_in, block)
+    balanced_relay(3, back, back_relay, back_in, block)
     token_pick = [pick_sum(value_expert, value_place, block, q * capacity, width) for q in range(4)]
     plane_wait(3, back, back_in, block)
     for q in range(4):
@@ -397,10 +472,10 @@
     value_weight_grad[...] = total[:, :head_size]
     output_weight_grad[...] = total[:, head_size:]
 
-    plane_drain(0, sent, held, block)
+    balanced_drain(0, sent, relay, held, block)
     plane_drain(1, answer, returned, small)
     plane_drain(2, gated, held_rows, small)
-    plane_drain(3, back, back_in, block)
+    balanced_drain(3, back, back_relay, back_in, block)
     pair_copy.wait_send()
 
     @pl.loop(1, chips)
@@ -411,6 +486,11 @@
     @pl.loop(0, chips)
     def _(j):
         forward_of(j).wait_send()
+
+
+def hand_over(*refs):
+    for source, target in zip(refs[:6], refs[6:]):
+        target[...] = source[...]
 
 
 def on_device(
@@ -433,7 +513,6 @@
     shard_rows = features // groups
     small = 48
     block = 4 * capacity
-    shard = jnp.concatenate([value_weight[0], output_weight[0]], axis=1)
     vmem = pl.BlockSpec(memory_space=pltpu.VMEM)
 
     def room(*shape):
@@ -445,15 +524,18 @@
             jax.ShapeDtypeStruct((tok_rows, features), BF16),
             jax.ShapeDtypeStruct((tok_rows, head_size), BF16),
             jax.ShapeDtypeStruct((tok_rows, head_size), BF16),
-            jax.ShapeDtypeStruct((tok_rows, 2 * experts), F32),
+            jax.ShapeDtypeStruct((2 * experts, tok_rows), F32),
             jax.ShapeDtypeStruct((shard_rows, head_size), F32),
             jax.ShapeDtypeStruct((shard_rows, head_size), F32),
         ),
-        in_specs=[vmem] * 8,
+        in_specs=[vmem] * 9,
         out_specs=(vmem,) * 6,
         scratch_shapes=[
+            room(shard_rows, 2 * head_size),
             room(experts * block, features // 2),
             room(experts * block, features // 2),
+            room(len(RELAYED), block, features // 2),
+            room(len(RELAYED), block, features // 4),
             room(features, 2 * head_size),
             room(features // 4, 4 * head_size),
             room(experts * small, head_size),
@@ -476,11 +558,29 @@
             pltpu.SemaphoreType.DMA((chips,)),
             pltpu.SemaphoreType.DMA,
             pltpu.SemaphoreType.DMA,
+            pltpu.SemaphoreType.DMA((2, len(RELAYED))),
+            pltpu.SemaphoreType.DMA((2, len(RELAYED))),
             pltpu.SemaphoreType.DMA((5,)),
         ],
         compiler_params=pltpu.CompilerParams(collective_id=0, has_side_effects=True),
-    )(tokens, queries, key_vectors, gate_logits, value_routes, output_routes, shard, cotangent)
-    return outs[:4] + (outs[4][None], outs[5][None])
+    )(
+        tokens,
+        queries,
+        key_vectors,
+        gate_logits.T,
+        value_routes.T,
+        output_routes.T,
+        value_weight,
+        output_weight,
+        cotangent,
+    )
+    outs = pl.pallas_call(
+        hand_over,
+        out_shape=tuple(jax.ShapeDtypeStruct(out.shape, out.dtype) for out in outs),
+        in_specs=[vmem] * 6,
+        out_specs=(vmem,) * 6,
+    )(*outs)
+    return outs[:3] + (outs[3].T, outs[4][None], outs[5][None])
 
 
 def solution(mesh):

time: 119 us -> 105 us (0.88)
  the two profiles are of different devices: /device:TPU:1 before, /device:TPU:33 now
where the time goes in v3:
time: 105 us
  Pallas kernels  105 us (100%)
    pallas_call x1, Pallas kernels, on_device(): pl.pallas_call(functools.partial(kernel, groups), out_shape=(jax.ShapeDty...  103 us

profile of v3, /device:TPU:33, one launch (start us, length us, event | category | flops | bytes accessed | tf_op | source)
XLA Modules:
  0.0 105.2 jit_solution(8273754526797175082)
XLA Ops:
  0.6 102.7 %shard_map.136 = (bf16[128,2048]{1,0:T(8,128)(2,1)}, bf16[128,128]{1,0:T(8,128)(2,1)}, bf16[128,128]{1,0:T(8,128)(2,1)}, f32[32,128]{1,0:T(8,128)}, f32[64,128]{1,0:T(8,128)}, /*index=5*/f32[64,128]{1,0:T(8,128)}) custom-call(bf16[128,2048]{1,0:T(8,128)(2,1)} %tokens.1, bf16[128,128]{1,0:T(8,128)(2,1)} %queries.1, bf16[128,128]{1,0:T(8,128)(2,1)} %key_vectors.1, ...), custom_call_target="tpu_custom_call" | custom-call | tf_op jit(solution)/shard_map/pallas_call | solution.py:521
  103.3 1.9 %shard_map.137 = (bf16[128,2048]{1,0:T(8,128)(2,1)}, bf16[128,128]{1,0:T(8,128)(2,1)}, bf16[128,128]{1,0:T(8,128)(2,1)}, f32[32,128]{1,0:T(8,128)}, f32[64,128]{1,0:T(8,128)}, /*index=5*/f32[64,128]{1,0:T(8,128)}) custom-call(bf16[128,2048]{1,0:T(8,128)(2,1)} %get-tuple-element.18.refs_0_, bf16[128,128]{1,0:T(8,128)(2,1)} %get-tuple-element.19.refs_1_, ...), custom_call_target="tpu_custom_call" | custom-call | tf_op jit(solution)/shard_map/pallas_call | solution.py:577

commit v4 on v3

--- a/solution.py
+++ b/solution.py
@@ -109,10 +109,12 @@
     value_weight_grad,
     output_weight_grad,
     shard,
+    chosen,
     sent,
     held,
     relay,
     back_relay,
+    sum_relay,
     banks,
     quarter_bank,
     answer,
@@ -137,6 +139,8 @@
     recv_p,
     send_r,
     recv_r,
+    send_q,
+    recv_q,
     local,
 ):
     tok_rows, features = tokens.shape
@@ -310,7 +314,7 @@
     value_stats = route_ranks(value_routes[...], experts)
     output_stats = route_ranks(output_routes[...], experts)
     width = experts * block
-    chosen = jnp.concatenate(
+    chosen[...] = jnp.concatenate(
         [
             chosen_rows(stats[:2], stats[2:], block, offset, width)
             for stats, offset in (
@@ -322,25 +326,34 @@
         ],
         axis=1,
     )
+    pl.semaphore_wait(barrier, experts - 1 + chips)
+    reach = chips // 4
+    for j in range(1, 2 * reach + 1):
+        shard_copy(j).start()
+    forward_copy(0, shard, me_dp).start()
     tile = 256
-    cut = width // 2
-    for c in range(half // tile):
-        low = pl.ds(c * tile, tile)
-        high = pl.ds(half + c * tile, tile)
-        rows = jnp.concatenate([tokens[:, low], cotangent[:, low], tokens[:, high], cotangent[:, high]], axis=0)
-        for part in range(2):
-            sent[part * cut : (part + 1) * cut, low] = contract(
-                chosen[part * cut : (part + 1) * cut, :], rows, ((1,), (0,))
-            ).astype(BF16)
-
-    pl.semaphore_wait(barrier, experts - 1 + chips)
-    balanced_start(0, sent, relay, held, block)
-
-    @pl.loop(1, chips)
-    def _(j):
-        shard_copy(j).start()
-
-    forward_copy(0, shard, me_dp).start()
+    stripe = SIDE * block
+
+    def stripe_of(index):
+        return pl.ds(pl.multiple_of(index * stripe, 16), stripe)
+
+    plane_order = (2, 1, 3, 0)
+    for dy in plane_order:
+        target_rows = stripe_of((y + dy) % SIDE)
+        for c in range(half // tile):
+            low = pl.ds(c * tile, tile)
+            high = pl.ds(half + c * tile, tile)
+            rows = jnp.concatenate(
+                [tokens[:, low], cotangent[:, low], tokens[:, high], cotangent[:, high]], axis=0
+            )
+            sent[target_rows, low] = contract(chosen[target_rows, :], rows, ((1,), (0,))).astype(BF16)
+        for r in range(len(RELAYED)):
+            if RELAYED[r][0][0] == dy:
+                first_leg(0, sent, relay, block, r).start()
+        for i in direct:
+            if i // SIDE == dy:
+                plane_copy(0, sent, held, block, i).start()
+    plane_own(0, sent, held, block).start()
     columns = jnp.concatenate(value_stats + output_stats, axis=0).T.astype(jnp.int32)
     value_expert, value_place, output_expert, output_place = [
         [columns[:, 2 * n + k : 2 * n + k + 1] for k in range(2)] for n in range(4)
@@ -355,9 +368,33 @@
         picks = [pick_rows(expert[k], place[k], stride, offset, width) for k in range(2)]
         return (picks[0] + picks[1]).astype(BF16)
 
+
+    def onward(j, via):
+        row = chip_source(via)
+        return pltpu.make_async_remote_copy(
+            src_ref=window(banks, row, shard_rows),
+            dst_ref=window(banks, row, shard_rows),
+            send_sem=send_z.at[0, j],
+            recv_sem=recv_z.at[0, j],
+            device_id={"dp": ((z + chip_step(j) + chips - chip_step(via)) % chips) * 2 + core},
+            device_id_type=MESH,
+        )
+
+    for via in (2 * reach - 1, 2 * reach):
+        shard_copy(via).wait_recv()
+        for j in range(2 * reach + 1, chips):
+            if j % 2 == via % 2:
+                onward(j, via).start()
+        forward_of(via).start()
+
+    @pl.loop(1, 2 * reach - 1)
+    def _(j):
+        shard_copy(j).wait_recv()
+        forward_of(j).start()
+
     balanced_relay(0, sent, relay, held, block)
 
-    @pl.loop(1, chips)
+    @pl.loop(2 * reach + 1, chips)
     def _(j):
         shard_copy(j).wait_recv()
         forward_of(j).start()
@@ -372,22 +409,32 @@
     for q in range(4):
         quarter_bank[:, q * head_size : (q + 1) * head_size] = banks[q * quarter : (q + 1) * quarter, :head_size]
 
-    plane_wait(0, sent, held, block)
-
     row_ids = lax.broadcasted_iota(jnp.int32, (2 * capacity, head_size), 0)
-    chunk = 4
-    for c in range(experts // chunk):
-        both = contract(held[c * chunk * block : (c + 1) * chunk * block, :], bank_pair, ((1,), (0,)))
+    chunk = SIDE
+    for dy in plane_order:
+        source_y = (y + SIDE - dy) % SIDE
+        for dx in range(SIDE):
+            if dy or dx:
+                plane_copy(0, sent, held, block, dy * SIDE + dx).wait_recv()
+            else:
+                plane_own(0, sent, held, block).wait()
+        both = contract(held[stripe_of(source_y), :], bank_pair, ((1,), (0,)))
+        blocks = []
         for k in range(chunk):
             top = both[k * block : k * block + 2 * capacity, : 2 * head_size]
             low = both[k * block + 2 * capacity : (k + 1) * block, 2 * head_size :]
             total = top + low
             rows = jnp.where(row_ids < capacity, total[:, :head_size], total[:, head_size:])
-            rows = jnp.concatenate([rows, jnp.zeros((small - 2 * capacity, head_size), F32)], axis=0)
-            e = c * chunk + k
-            answer[e * small : (e + 1) * small, :] = rows.astype(BF16)
-
-    plane_start(1, answer, returned, small)
+            blocks += [rows, jnp.zeros((small - 2 * capacity, head_size), F32)]
+        spot = pl.ds(pl.multiple_of(source_y * SIDE * small, 16), SIDE * small)
+        answer[spot, :] = jnp.concatenate(blocks, axis=0).astype(BF16)
+        for dx in range(SIDE):
+            i = ((SIDE - dy) % SIDE) * SIDE + dx
+            if i:
+                plane_copy(1, answer, returned, small, i).start()
+            else:
+                plane_own(1, answer, returned, small).start()
+
     value_pick = [
         pick_rows(value_expert[k], value_place[k], small, 0, experts * small).astype(BF16) for k in range(2)
     ]
@@ -446,12 +493,32 @@
     for k in range(chips):
         staged[k] = (parts[core, k].astype(F32) + pair[k].astype(F32)).astype(BF16)
 
-    @pl.loop(1, chips)
+    @pl.loop(1, chips - 1)
     def _(j):
         sum_copy(j).start()
 
+    quarter_turn = reach + core * (chips // 2)
+    far_first = pltpu.make_async_remote_copy(
+        src_ref=staged.at[(z + chips // 2) % chips],
+        dst_ref=sum_relay,
+        send_sem=send_z.at[1, chips - 1],
+        recv_sem=recv_q,
+        device_id={"dp": ((z + quarter_turn) % chips) * 2 + core},
+        device_id_type=MESH,
+    )
+    far_last = pltpu.make_async_remote_copy(
+        src_ref=sum_relay,
+        dst_ref=landed.at[(z + chips - quarter_turn) % chips],
+        send_sem=send_q,
+        recv_sem=recv_z.at[1, chips - 1],
+        device_id={"dp": ((z + quarter_turn) % chips) * 2 + core},
+        device_id_type=MESH,
+    )
+    far_first.start()
     balanced_start(3, back, back_relay, back_in, block)
     balanced_relay(3, back, back_relay, back_in, block)
+    far_first.wait_recv()
+    far_last.start()
     token_pick = [pick_sum(value_expert, value_place, block, q * capacity, width) for q in range(4)]
     plane_wait(3, back, back_in, block)
     for q in range(4):
@@ -477,6 +544,7 @@
     plane_drain(2, gated, held_rows, small)
     balanced_drain(3, back, back_relay, back_in, block)
     pair_copy.wait_send()
+    far_last.wait_send()
 
     @pl.loop(1, chips)
     def _(j):
@@ -532,10 +600,12 @@
         out_specs=(vmem,) * 6,
         scratch_shapes=[
             room(shard_rows, 2 * head_size),
+            room(experts * block, 4 * tok_rows),
             room(experts * block, features // 2),
             room(experts * block, features // 2),
             room(len(RELAYED), block, features // 2),
             room(len(RELAYED), block, features // 4),
+            room(shard_rows, 2 * head_size),
             room(features, 2 * head_size),
             room(features // 4, 4 * head_size),
             room(experts * small, head_size),
@@ -560,6 +630,8 @@
             pltpu.SemaphoreType.DMA,
             pltpu.SemaphoreType.DMA((2, len(RELAYED))),
             pltpu.SemaphoreType.DMA((2, len(RELAYED))),
+            pltpu.SemaphoreType.DMA,
+            pltpu.SemaphoreType.DMA,
             pltpu.SemaphoreType.DMA((5,)),
         ],
         compiler_params=pltpu.CompilerParams(collective_id=0, has_side_effects=True),

time: 105 us -> 110 us (1.048)
  the two profiles are of different devices: /device:TPU:33 before, /device:TPU:1 now
where the time goes in v4:
time: 110 us; the launch traced here: 109 us
  Pallas kernels  108 us (98%)
    pallas_call x1, Pallas kernels, on_device(): pl.pallas_call(functools.partial(kernel, groups), out_shape=(jax.ShapeDty...  106 us

profile of v4, /device:TPU:1, one launch (start us, length us, event | category | flops | bytes accessed | tf_op | source)
XLA Modules:
  0.0 108.8 jit_solution(6093004467394797945)
XLA Ops:
  0.6 106.2 %shard_map.136 = (bf16[128,2048]{1,0:T(8,128)(2,1)}, bf16[128,128]{1,0:T(8,128)(2,1)}, bf16[128,128]{1,0:T(8,128)(2,1)}, f32[32,128]{1,0:T(8,128)}, f32[64,128]{1,0:T(8,128)}, /*index=5*/f32[64,128]{1,0:T(8,128)}) custom-call(bf16[128,2048]{1,0:T(8,128)(2,1)} %tokens.1, bf16[128,128]{1,0:T(8,128)(2,1)} %queries.1, bf16[128,128]{1,0:T(8,128)(2,1)} %key_vectors.1, ...), custom_call_target="tpu_custom_call" | custom-call | tf_op jit(solution)/shard_map/pallas_call | solution.py:589
  106.9 1.9 %shard_map.137 = (bf16[128,2048]{1,0:T(8,128)(2,1)}, bf16[128,128]{1,0:T(8,128)(2,1)}, bf16[128,128]{1,0:T(8,128)(2,1)}, f32[32,128]{1,0:T(8,128)}, f32[64,128]{1,0:T(8,128)}, /*index=5*/f32[64,128]{1,0:T(8,128)}) custom-call(bf16[128,2048]{1,0:T(8,128)(2,1)} %get-tuple-element.18.refs_0_, bf16[128,128]{1,0:T(8,128)(2,1)} %get-tuple-element.19.refs_1_, ...), custom_call_target="tpu_custom_call" | custom-call | tf_op jit(solution)/shard_map/pallas_call | solution.py:649

commit v5 on v4

--- a/solution.py
+++ b/solution.py
@@ -114,7 +114,6 @@
     held,
     relay,
     back_relay,
-    sum_relay,
     banks,
     quarter_bank,
     answer,
@@ -139,8 +138,6 @@
     recv_p,
     send_r,
     recv_r,
-    send_q,
-    recv_q,
     local,
 ):
     tok_rows, features = tokens.shape
@@ -326,11 +323,7 @@
         ],
         axis=1,
     )
-    pl.semaphore_wait(barrier, experts - 1 + chips)
     reach = chips // 4
-    for j in range(1, 2 * reach + 1):
-        shard_copy(j).start()
-    forward_copy(0, shard, me_dp).start()
     tile = 256
     stripe = SIDE * block
 
@@ -347,6 +340,11 @@
                 [tokens[:, low], cotangent[:, low], tokens[:, high], cotangent[:, high]], axis=0
             )
             sent[target_rows, low] = contract(chosen[target_rows, :], rows, ((1,), (0,))).astype(BF16)
+        if dy == plane_order[0]:
+            pl.semaphore_wait(barrier, experts - 1 + chips)
+            for j in range(2 * reach, 0, -1):
+                shard_copy(j).start()
+            forward_copy(0, shard, me_dp).start()
         for r in range(len(RELAYED)):
             if RELAYED[r][0][0] == dy:
                 first_leg(0, sent, relay, block, r).start()
@@ -387,12 +385,12 @@
                 onward(j, via).start()
         forward_of(via).start()
 
+    balanced_relay(0, sent, relay, held, block)
+
     @pl.loop(1, 2 * reach - 1)
     def _(j):
         shard_copy(j).wait_recv()
         forward_of(j).start()
-
-    balanced_relay(0, sent, relay, held, block)
 
     @pl.loop(2 * reach + 1, chips)
     def _(j):
@@ -493,32 +491,12 @@
     for k in range(chips):
         staged[k] = (parts[core, k].astype(F32) + pair[k].astype(F32)).astype(BF16)
 
-    @pl.loop(1, chips - 1)
+    @pl.loop(1, chips)
     def _(j):
         sum_copy(j).start()
 
-    quarter_turn = reach + core * (chips // 2)
-    far_first = pltpu.make_async_remote_copy(
-        src_ref=staged.at[(z + chips // 2) % chips],
-        dst_ref=sum_relay,
-        send_sem=send_z.at[1, chips - 1],
-        recv_sem=recv_q,
-        device_id={"dp": ((z + quarter_turn) % chips) * 2 + core},
-        device_id_type=MESH,
-    )
-    far_last = pltpu.make_async_remote_copy(
-        src_ref=sum_relay,
-        dst_ref=landed.at[(z + chips - quarter_turn) % chips],
-        send_sem=send_q,
-        recv_sem=recv_z.at[1, chips - 1],
-        device_id={"dp": ((z + quarter_turn) % chips) * 2 + core},
-        device_id_type=MESH,
-    )
-    far_first.start()
     balanced_start(3, back, back_relay, back_in, block)
     balanced_relay(3, back, back_relay, back_in, block)
-    far_first.wait_recv()
-    far_last.start()
     token_pick = [pick_sum(value_expert, value_place, block, q * capacity, width) for q in range(4)]
     plane_wait(3, back, back_in, block)
     for q in range(4):
@@ -544,7 +522,6 @@
     plane_drain(2, gated, held_rows, small)
     balanced_drain(3, back, back_relay, back_in, block)
     pair_copy.wait_send()
-    far_last.wait_send()
 
     @pl.loop(1, chips)
     def _(j):
@@ -605,7 +582,6 @@
             room(experts * block, features // 2),
             room(len(RELAYED), block, features // 2),
             room(len(RELAYED), block, features // 4),
-            room(shard_rows, 2 * head_size),
             room(features, 2 * head_size),
             room(features // 4, 4 * head_size),
             room(experts * small, head_size),
@@ -630,8 +606,6 @@
             pltpu.SemaphoreType.DMA,
             pltpu.SemaphoreType.DMA((2, len(RELAYED))),
             pltpu.SemaphoreType.DMA((2, len(RELAYED))),
-            pltpu.SemaphoreType.DMA,
-            pltpu.SemaphoreType.DMA,
             pltpu.SemaphoreType.DMA((5,)),
         ],
         compiler_params=pltpu.CompilerParams(collective_id=0, has_side_effects=True),

time: 110 us -> 106 us (0.964)
  the two profiles are of different devices: /device:TPU:1 before, /device:TPU:33 now
where the time goes in v5:
time: 106 us
  Pallas kernels  106 us (100%)
    pallas_call x1, Pallas kernels, on_device(): pl.pallas_call(functools.partial(kernel, groups), out_shape=(jax.ShapeDty...  104 us

profile of v5, /device:TPU:33, one launch (start us, length us, event | category | flops | bytes accessed | tf_op | source)
XLA Modules:
  0.0 106.2 jit_solution(6672344483492530065)
XLA Ops:
  0.6 103.6 %shard_map.136 = (bf16[128,2048]{1,0:T(8,128)(2,1)}, bf16[128,128]{1,0:T(8,128)(2,1)}, bf16[128,128]{1,0:T(8,128)(2,1)}, f32[32,128]{1,0:T(8,128)}, f32[64,128]{1,0:T(8,128)}, /*index=5*/f32[64,128]{1,0:T(8,128)}) custom-call(bf16[128,2048]{1,0:T(8,128)(2,1)} %tokens.1, bf16[128,128]{1,0:T(8,128)(2,1)} %queries.1, bf16[128,128]{1,0:T(8,128)(2,1)} %key_vectors.1, ...), custom_call_target="tpu_custom_call" | custom-call | tf_op jit(solution)/shard_map/pallas_call | solution.py:566
  104.2 1.9 %shard_map.137 = (bf16[128,2048]{1,0:T(8,128)(2,1)}, bf16[128,128]{1,0:T(8,128)(2,1)}, bf16[128,128]{1,0:T(8,128)(2,1)}, f32[32,128]{1,0:T(8,128)}, f32[64,128]{1,0:T(8,128)}, /*index=5*/f32[64,128]{1,0:T(8,128)}) custom-call(bf16[128,2048]{1,0:T(8,128)(2,1)} %get-tuple-element.18.refs_0_, bf16[128,128]{1,0:T(8,128)(2,1)} %get-tuple-element.19.refs_1_, ...), custom_call_target="tpu_custom_call" | custom-call | tf_op jit(solution)/shard_map/pallas_call | solution.py:623

commit v6 on v3

--- a/solution.py
+++ b/solution.py
@@ -334,11 +334,10 @@
             ).astype(BF16)
 
     pl.semaphore_wait(barrier, experts - 1 + chips)
+    reach = chips // 4
+    for j in range(2 * reach, 0, -1):
+        shard_copy(j).start()
     balanced_start(0, sent, relay, held, block)
-
-    @pl.loop(1, chips)
-    def _(j):
-        shard_copy(j).start()
 
     forward_copy(0, shard, me_dp).start()
     columns = jnp.concatenate(value_stats + output_stats, axis=0).T.astype(jnp.int32)
@@ -355,9 +354,32 @@
         picks = [pick_rows(expert[k], place[k], stride, offset, width) for k in range(2)]
         return (picks[0] + picks[1]).astype(BF16)
 
+    def onward(j, via):
+        row = chip_source(via)
+        return pltpu.make_async_remote_copy(
+            src_ref=window(banks, row, shard_rows),
+            dst_ref=window(banks, row, shard_rows),
+            send_sem=send_z.at[0, j],
+            recv_sem=recv_z.at[0, j],
+            device_id={"dp": ((z + chip_step(j) + chips - chip_step(via)) % chips) * 2 + core},
+            device_id_type=MESH,
+        )
+
+    for via in (2 * reach - 1, 2 * reach):
+        shard_copy(via).wait_recv()
+        for j in range(2 * reach + 1, chips):
+            if j % 2 == via % 2:
+                onward(j, via).start()
+        forward_of(via).start()
+
     balanced_relay(0, sent, relay, held, block)
 
-    @pl.loop(1, chips)
+    @pl.loop(1, 2 * reach - 1)
+    def _(j):
+        shard_copy(j).wait_recv()
+        forward_of(j).start()
+
+    @pl.loop(2 * reach + 1, chips)
     def _(j):
         shard_copy(j).wait_recv()
         forward_of(j).start()

time: 105 us -> 105 us (level)
  no operation moved by 1% of the time
where the time goes in v6:
time: 105 us
  Pallas kernels  105 us (100%)
    pallas_call x1, Pallas kernels, on_device(): pl.pallas_call(functools.partial(kernel, groups), out_shape=(jax.ShapeDty...  103 us

profile of v6, /device:TPU:33, one launch (start us, length us, event | category | flops | bytes accessed | tf_op | source)
XLA Modules:
  0.0 105.2 jit_solution(4243789787881465289)
XLA Ops:
  0.6 102.7 %shard_map.136 = (bf16[128,2048]{1,0:T(8,128)(2,1)}, bf16[128,128]{1,0:T(8,128)(2,1)}, bf16[128,128]{1,0:T(8,128)(2,1)}, f32[32,128]{1,0:T(8,128)}, f32[64,128]{1,0:T(8,128)}, /*index=5*/f32[64,128]{1,0:T(8,128)}) custom-call(bf16[128,2048]{1,0:T(8,128)(2,1)} %tokens.1, bf16[128,128]{1,0:T(8,128)(2,1)} %queries.1, bf16[128,128]{1,0:T(8,128)(2,1)} %key_vectors.1, ...), custom_call_target="tpu_custom_call" | custom-call | tf_op jit(solution)/shard_map/pallas_call | solution.py:543
  103.3 1.9 %shard_map.137 = (bf16[128,2048]{1,0:T(8,128)(2,1)}, bf16[128,128]{1,0:T(8,128)(2,1)}, bf16[128,128]{1,0:T(8,128)(2,1)}, f32[32,128]{1,0:T(8,128)}, f32[64,128]{1,0:T(8,128)}, /*index=5*/f32[64,128]{1,0:T(8,128)}) custom-call(bf16[128,2048]{1,0:T(8,128)(2,1)} %get-tuple-element.18.refs_0_, bf16[128,128]{1,0:T(8,128)(2,1)} %get-tuple-element.19.refs_1_, ...), custom_call_target="tpu_custom_call" | custom-call | tf_op jit(solution)/shard_map/pallas_call | solution.py:599
